TPU v7x, 512 devices: a whole 4x8x8 slice. The times are simulated.
512 devices in a mesh: grp: 16 (over y, core), mem: 32 (over x, z).
Axes of the slice: x: 4, y: 8, z: 8, core: 2. Of those that a mesh axis runs over, the one named last changes fastest.
Arguments:
- spectral: bfloat16 [512, 3, 2, 256, 192], P('grp', None, None, 'mem'), may hold values from -6 to 6
- inverse: bfloat16 [512, 192, 192], P('grp'), may hold values from -0.4375 to 0.4375
- legendre: bfloat16 [256, 256, 512], P('mem', None, 'grp'), may hold values from -0.015625 to 0.015625
- vorticity: bfloat16 [3, 256, 192, 1536], P(None, 'mem', 'grp'), may hold values from -6 to 6
- degree_list: int32 [512], replicated, may hold values from 0 to 511, as said below
- order_map: int32 [256], replicated, may hold values from 0 to 255, as said below
Outputs:
- advection: bfloat16 [3, 256, 192, 1536], P(None, 'mem', 'grp')
Inputs may be any that keep to these rules, and one draw needn't show every extreme that they name: `degree_list`: a permutation of the degrees; slots 2j and 2j + 1 hold a degree d and 511 - d. `order_map`: a permutation of the orders; slots 2j and 2j + 1 hold an order m and 255 - m.
All inputs are finite; a program needn't handle non-finite values.
Results may differ from a plain program's by a relative error of at most 0.0062.
Values may be sent and summed in bfloat16 or wider, within the bound.
No kernel may reach another device: no remote copies, remote signals or barrier semaphores. Data moves between devices by JAX's collectives and lax.ppermute only.
A program may use at most 64 MiB of HBM per device.

v0:
```python
import math

import jax
import jax.numpy as jnp
from jax import lax
from jax.sharding import PartitionSpec as P


def cross_product(flow_velocity, vorticity):
    other = vorticity.astype(jnp.float32)
    first = flow_velocity[:, :, 1] * other[2] - flow_velocity[:, :, 2] * other[1]
    second = flow_velocity[:, :, 2] * other[0] - flow_velocity[:, :, 0] * other[2]
    third = flow_velocity[:, :, 0] * other[1] - flow_velocity[:, :, 1] * other[0]
    return jnp.stack([first, second, third]).astype(jnp.bfloat16)


def fourier_table(order_map, count):
    longitude = jnp.arange(count, dtype=jnp.int32)
    phase = order_map[:, None] * longitude[None, :] % count
    angle = phase.astype(jnp.float32) * (2.0 * math.pi / count)
    weight = jnp.where(order_map == 0, 1.0, 2.0).astype(jnp.float32)[:, None]
    return jnp.stack([weight * jnp.cos(angle), -weight * jnp.sin(angle)], axis=1).astype(
        jnp.bfloat16
    )


def solve_radial(rows, profiles):
    width_now = profiles.shape[0]
    orders_here = profiles.shape[3]
    flat_profiles = profiles.reshape(width_now, 6 * orders_here, profiles.shape[4])
    solved = lax.dot_general(
        rows, flat_profiles, (((2,), (2,)), ((0,), (0,))), preferred_element_type=jnp.float32
    )
    return solved.astype(jnp.bfloat16)


def order_major(values, orders_here):
    width_now = values.shape[0]
    shells_now = values.shape[1]
    return jnp.transpose(values.reshape(width_now, shells_now * 6, orders_here), (2, 0, 1))


def legendre_term(segment, block, degree_list, local_order_list):
    allowed = local_order_list[:, None] <= degree_list[None, :]
    table = jnp.where(allowed[:, None, :], segment, jnp.zeros_like(segment))
    product = lax.dot_general(
        table, block, (((2,), (1,)), ((0,), (0,))), preferred_element_type=jnp.float32
    )
    return product


def shards(spectral, inverse, legendre, vorticity, degree_list, order_map):
    member_order_list = spectral.shape[3]
    member_shell_rows = vorticity.shape[2]
    member_index = lax.axis_index("mem")
    local_order_list = lax.dynamic_slice_in_dim(
        order_map, member_index * member_order_list, member_order_list
    )
    radial_factor = solve_radial(inverse, spectral)
    moved = lax.all_to_all(radial_factor, "grp", split_axis=1, concat_axis=0, tiled=True)
    by_order = order_major(moved, member_order_list)
    merged_value_rows = legendre_term(
        lax.all_gather(legendre, "grp", axis=2, tiled=True), by_order, degree_list, local_order_list
    )
    latitudinal = merged_value_rows.astype(jnp.bfloat16)
    gathered = lax.all_to_all(latitudinal, "mem", split_axis=1, concat_axis=0, tiled=True)
    complete_order_list = gathered.shape[0]
    member_latitude_rows = gathered.shape[1]
    arranged = gathered.reshape(complete_order_list, member_latitude_rows, member_shell_rows, 3, 2)
    trig = fourier_table(order_map, vorticity.shape[3])
    flow_velocity = jnp.einsum(
        "mtsck,mkp->tscp", arranged, trig, preferred_element_type=jnp.float32
    )
    return cross_product(flow_velocity, vorticity)


def solution(mesh):
    return jax.shard_map(
        shards,
        mesh=mesh,
        in_specs=(
            P("grp", None, None, "mem", None),
            P("grp", None, None),
            P("mem", None, "grp"),
            P(None, "mem", "grp", None),
            P(),
            P(),
        ),
        out_specs=P(None, "mem", "grp", None),
        check_vma=False,
    )
```

profile of v0, /device:TPU:1, one launch (start us, length us, event | category | flops | bytes accessed | tf_op | source)
XLA Modules:
  0.0 122.5 jit_solution(2055833238189839001)
XLA Ops:
  6.5 0.0 copy-start
  6.5 0.0 all-gather.2.cloned.1.call-start
  6.5 0.7 all-gather.2.cloned.1.call-update
  7.3 1.2 copy-done
  8.4 3.1 %convolution_convert_fusion = bf16[32,192,48]{1,2,0:T(8,128)(2,1)} fusion(bf16[32,192,192]{2,1,0:T(8,128)(2,1)S(1)} %copy-done, bf16[32,48,192]{2,1,0:T(8,128)(2,1)} %bitcast.54), kind=kOutput, calls=%fused_computation.16 | convolution fusion | flops 113541120 | bytes 3538944 | tf_op jit(solution)/shard_map/dot_general | solution.py:31
  11.5 3.1 %copy.23 = bf16[32,192,48]{2,0,1:T(8,128)(2,1)} copy(bf16[32,192,48]{1,2,0:T(8,128)(2,1)} %convolution_convert_fusion) | data formatting | bytes 1179648 | tf_op jit(solution)/shard_map/convert_element_type | solution.py:34
  14.7 4.2 %reshape.164 = bf16[16,2,9216]{2,1,0:T(2,128)(2,1)} reshape(bf16[192,32,48]{2,1,0:T(8,128)(2,1)} %bitcast.52) | data formatting | bytes 1179648
  18.8 10.8 %all-to-all-start = ((bf16[16,2,9216]{2,1,0:T(2,128)(2,1)}), bf16[16,2,9216]{2,1,0:T(2,128)(2,1)}, u32[]{:S(2)}, u32[]{:S(2)}) async-start(bf16[16,2,9216]{2,1,0:T(2,128)(2,1)} %reshape.164), calls=%async_computation | async-start | bytes 1179648 | tf_op jit(solution)/shard_map/all_to_all | solution.py:60
  29.7 0.0 copy-done.3
  29.7 0.1 dynamic_slice.3
  29.8 0.0 copy-done.4
  29.8 0.1 broadcast_compare_fusion
  29.8 22.7 %all-to-all-done = bf16[16,2,9216]{2,1,0:T(2,128)(2,1)} async-done(((bf16[16,2,9216]{2,1,0:T(2,128)(2,1)}), bf16[16,2,9216]{2,1,0:T(2,128)(2,1)}, u32[]{:S(2)}, u32[]{:S(2)}) %all-to-all-start) | async-done | bytes 589856 | tf_op jit(solution)/shard_map/all_to_all | solution.py:60
  52.6 3.4 %reshape.165 = bf16[192,32,48]{2,1,0:T(8,128)(2,1)} reshape(bf16[16,2,9216]{2,1,0:T(2,128)(2,1)} %all-to-all-done) | data formatting | bytes 1179648
  55.9 4.4 %copy.24 = bf16[16,32,12,48]{1,0,3,2:T(8,128)(2,1)} copy(bf16[16,32,12,48]{3,1,2,0:T(8,128)(2,1)} %bitcast.53) | data formatting | bytes 1179648 | tf_op jit(solution)/shard_map/all_to_all | solution.py:60
  60.4 4.5 %reshape.160 = bf16[512,72,8]{0,2,1:T(8,128)(2,1)} reshape(bf16[16,32,12,48]{1,0,3,2:T(8,128)(2,1)} %copy.24) | data formatting | bytes 1179648 | tf_op jit(solution)/shard_map/reshape | solution.py:40
  64.8 2.5 %fusion.10 = bf16[8,256,72]{1,2,0:T(8,128)(2,1)S(1)} fusion(bf16[8,256,512]{1,2,0:T(8,128)(2,1)} %all-gather.2.cloned.1.call-done, pred[8,512]{1,0:T(8,128)(4,1)S(1)} %broadcast_compare_fusion, bf16[512,72,8]{0,2,1:T(8,128)(2,1)} %reshape.160), kind=kOutput, calls=%fused_computation.17 | convolution fusion | flops 152190976 | bytes 2985984 | tf_op jit(solution)/shard_map/dot_general | solution.py:46
  67.3 1.1 copy.27
  68.4 10.8 %all-to-all-start.1 = ((bf16[8,256,72]{2,0,1:T(8,128)(2,1)}), bf16[8,256,72]{2,0,1:T(8,128)(2,1)}, u32[]{:S(2)}, u32[]{:S(2)}) async-start(bf16[8,256,72]{2,0,1:T(8,128)(2,1)} %copy.27), calls=%async_computation.1 | async-start | bytes 1048576 | tf_op jit(solution)/shard_map/all_to_all | solution.py:66
  79.3 0.0 copy-start.2
  79.3 7.9 %multiply_convert_fusion.1 = (bf16[256,1,1536]{2,0,1:T(8,128)(2,1)}, bf16[256,1,1536]{2,0,1:T(8,128)(2,1)}) fusion(s32[256]{0:T(256)S(1)} %copy-done.3, f32[256]{0:T(256)S(1)} %get-tuple-element.10, f32[256]{0:T(256)S(1)} %get-tuple-element.11), kind=kLoop, calls=%fused_computation.11 | loop fusion | flops 5111808 | bytes 1575936 | tf_op jit(solution)/shard_map/convert.3
  87.2 0.0 copy-done.2
  87.2 1.8 %copy_convert_fusion = f32[3,8,12,1536]{3,2,1,0:T(8,128)} fusion(bf16[3,8,12,1536]{3,1,2,0:T(8,128)(2,1)S(1)} %copy-done.2), kind=kLoop, calls=%fused_computation.19 | loop fusion | flops 442368 | bytes 2654208 | tf_op jit(solution)/shard_map/convert_element_type | solution.py:10
  89.0 6.4 %all-to-all-done.1 = bf16[8,256,72]{2,0,1:T(8,128)(2,1)} async-done(((bf16[8,256,72]{2,0,1:T(8,128)(2,1)}), bf16[8,256,72]{2,0,1:T(8,128)(2,1)}, u32[]{:S(2)}, u32[]{:S(2)}) %all-to-all-start.1) | async-done | bytes 294944 | tf_op jit(solution)/shard_map/all_to_all | solution.py:66
  95.4 8.4 %copy.29 = bf16[32,8,8,72]{1,0,2,3:T(8,128)(2,1)} copy(bf16[32,8,8,72]{3,1,2,0:T(8,128)(2,1)} %bitcast.6) | data formatting | bytes 589824 | tf_op jit(solution)/shard_map/all_to_all | solution.py:66
  103.8 7.3 %reshape.161 = bf16[256,8,12,3,2]{0,1,4,3,2:T(8,128)(2,1)S(1)} reshape(bf16[32,8,8,72]{1,0,2,3:T(8,128)(2,1)} %copy.29) | data formatting | bytes 589824 | tf_op jit(solution)/shard_map/reshape | solution.py:69
  111.2 0.0 copy-start.1
  111.2 2.3 %convolution_bitcast_fusion = f32[8,12,3,1536]{3,1,2,0:T(8,128)S(1)} fusion(bf16[256,1,1536]{2,0,1:T(8,128)(2,1)} %get-tuple-element.9, bf16[256,1,1536]{2,0,1:T(8,128)(2,1)} %get-tuple-element.8, bf16[256,8,12,3,2]{0,1,4,3,2:T(8,128)(2,1)S(1)} %reshape.161), kind=kOutput, calls=%fused_computation | convolution fusion | flops 453771264 | bytes 3637248 | tf_op jit(solution)/shard_map/mtsck,mkp->tscp/dot_general | solution.py:71
  113.5 0.0 copy-done.1
  113.5 0.6 subtract_convert_fusion.2
  114.1 0.2 pad_maximum_fusion
  114.3 1.4 %copy.34 = bf16[3,8,12,1536]{3,1,2,0:T(8,128)(2,1)} copy(bf16[3,8,12,1536]{3,2,1,0:T(8,128)(2,1)S(1)} %pad_maximum_fusion) | data formatting | bytes 1769472 | tf_op jit(solution)/shard_map/stack | solution.py:14
  (4 shorter events, 0.0 us)
Async XLA Ops:
  6.5 1.9 %copy-start = (bf16[32,192,192]{2,1,0:T(8,128)(2,1)S(1)}, bf16[32,192,192]{2,1,0:T(8,128)(2,1)}, u32[]{:S(2)}) copy-start(bf16[32,192,192]{2,1,0:T(8,128)(2,1)} %param.7) | copy-start | bytes 7077892
  6.5 58.3 %all-gather.2.cloned.1.call-start = ((), (), s32[]{:S(2)}) async-start(), calls=%async_computation.2 | async-start | bytes 2228224 | tf_op jit(solution)/shard_map/all_gather | solution.py:63
  14.7 15.0 %copy-start.3 = (s32[256]{0:T(256)S(1)}, s32[256]{0:T(256)}, u32[]{:S(2)}) copy-start(s32[256]{0:T(256)} %param.11) | copy-start | bytes 3076
  14.7 15.1 %copy-start.4 = (s32[512]{0:T(512)S(1)}, s32[512]{0:T(512)}, u32[]{:S(2)}) copy-start(s32[512]{0:T(512)} %param.10) | copy-start | bytes 6148
  18.8 33.7 %all-to-all-start = ((bf16[16,2,9216]{2,1,0:T(2,128)(2,1)}), bf16[16,2,9216]{2,1,0:T(2,128)(2,1)}, u32[]{:S(2)}, u32[]{:S(2)}) async-start(bf16[16,2,9216]{2,1,0:T(2,128)(2,1)} %reshape.164), calls=%async_computation | async-start | bytes 1179648 | tf_op jit(solution)/shard_map/all_to_all | solution.py:60
  68.4 27.0 %all-to-all-start.1 = ((bf16[8,256,72]{2,0,1:T(8,128)(2,1)}), bf16[8,256,72]{2,0,1:T(8,128)(2,1)}, u32[]{:S(2)}, u32[]{:S(2)}) async-start(bf16[8,256,72]{2,0,1:T(8,128)(2,1)} %copy.27), calls=%async_computation.1 | async-start | bytes 1048576 | tf_op jit(solution)/shard_map/all_to_all | solution.py:66
  79.3 7.9 %copy-start.2 = (bf16[3,8,12,1536]{3,1,2,0:T(8,128)(2,1)S(1)}, bf16[3,8,12,1536]{3,1,2,0:T(8,128)(2,1)}, u32[]{:S(2)}) copy-start(bf16[3,8,12,1536]{3,1,2,0:T(8,128)(2,1)} %param.9) | copy-start | bytes 2654212
  111.2 2.3 %copy-start.1 = (f32[3,8,12,1536]{3,2,1,0:T(8,128)S(1)}, f32[3,8,12,1536]{3,2,1,0:T(8,128)}, u32[]{:S(2)}) copy-start(f32[3,8,12,1536]{3,2,1,0:T(8,128)} %copy_convert_fusion) | copy-start | bytes 5308420
Sparse Core Ops, SparseCore 0:
  9.5 53.3 all-gather.1
where the time goes:
time: 123 us
  local copies, waits for them, and re-layouts  39 us (32%)
  waiting for transfers between devices  29.8 us (24%)
  starting transfers between devices  21.7 us (18%)
  between operations  13.5 us (11%)
  other arithmetic  10.6 us (9%)
  matrix products  7.9 us (6%)
    all_to_all x1, waiting for transfers between devices, shards(): lax.all_to_all(radial_factor, 'grp', split_axis=1, concat_axis=0, tiled=T...  22.7 us
    all_to_all x1, starting transfers between devices, shards(): lax.all_to_all(latitudinal, 'mem', split_axis=1, concat_axis=0, tiled=True)  10.8 us
    all_to_all x1, starting transfers between devices, shards(): lax.all_to_all(radial_factor, 'grp', split_axis=1, concat_axis=0, tiled=T...  10.8 us
    unnamed x12, local copies, waits for them, and re-layouts  8.73 us
    another operation x2, other arithmetic  8.55 us
    all_to_all x1, local copies, waits for them, and re-layouts, shards(): lax.all_to_all(latitudinal, 'mem', split_axis=1, concat_axis=0, tiled=True)  8.4 us
    reshape x1, local copies, waits for them, and re-layouts, shards(): gathered.reshape(complete_order_list, member_latitude_rows, member_shell_...  7.31 us
    all_to_all x1, waiting for transfers between devices, shards(): lax.all_to_all(latitudinal, 'mem', split_axis=1, concat_axis=0, tiled=True)  6.42 us
  transfers between devices with their start and end apart: 3, of which 2 were waited for; matrix products, arithmetic and copies ran while one was open for 27% of the time, Pallas kernels for 0%

commit v1 on v0

v1 whole, which is shorter than its diff:
```python
import math

import jax
import jax.numpy as jnp
from jax import lax
from jax.experimental import pallas as pl
from jax.experimental.pallas import tpu as pltpu
from jax.sharding import Mesh
from jax.sharding import PartitionSpec as P

YS, YM, CORES = 2, 4, 2
CHIPS = YS * YM
F32, BF16 = jnp.float32, jnp.bfloat16


def dot(left, right, contract):
    return lax.dot_general(left, right, ((contract[:1], contract[1:]), ((), ())), preferred_element_type=F32)


def trig_tables(orders, count):
    longitude = jnp.arange(count, dtype=jnp.int32)
    phase = orders[:, None] * longitude[None, :] % count
    angle = phase.astype(F32) * (2.0 * math.pi / count)
    weight = jnp.where(orders == 0, 1.0, 2.0).astype(F32)[:, None]
    return (weight * jnp.cos(angle)).astype(BF16), (-weight * jnp.sin(angle)).astype(BF16)


def one_hot_rows(targets, width):
    return (targets[:, None] == jnp.arange(width, dtype=jnp.int32)[None, :]).astype(BF16)


def iota(shape, axis):
    return lax.broadcasted_iota(jnp.int32, shape, axis)


def pack_kernel(spec_ref, inv_ref, leg_ref, out_ref, solved_ref):
    degrees = spec_ref.shape[0]
    rows = degrees * 8
    for l in range(degrees):
        product = dot(spec_ref[l], inv_ref[l], (1, 1))
        for ck in range(6):
            solved_ref[ck, l * 8 : (l + 1) * 8, :] = product[ck * 8 : (ck + 1) * 8, :]
    r, c = iota((rows, rows), 0), iota((rows, rows), 1)
    swap = (c == r % degrees * 8 + r // degrees).astype(BF16)
    by_order = [dot(swap, solved_ref[ck].astype(BF16), (1, 0)) for ck in range(6)]
    half = by_order[0].shape[1] // YS
    for ys in range(YS):
        parts = [v[:, ys * half : (ys + 1) * half] for v in by_order]
        parts.append(jnp.zeros((rows, out_ref.shape[3] - 256 - 6 * half), F32))
        radial = jnp.concatenate(parts, axis=1).astype(BF16)
        for ym in range(YM):
            for o in range(2):
                at = (ym * 2 + o) * degrees
                out_ref[ys * YM + ym, o, :, 256:] = radial[at : at + degrees, :]
    r, c = iota((256, 256), 0), iota((256, 256), 1)
    turn = (r == c % 32 * 8 + c // 32).astype(BF16)
    table = dot(leg_ref[...].reshape(rows, 256), turn, (1, 0)).astype(BF16)
    for ym in range(YM):
        for o in range(2):
            at = (ym * 2 + o) * degrees
            for ys in range(YS):
                out_ref[ys * YM + ym, o, :, :256] = table[at : at + degrees, :]


def pack(spectral, inverse, legendre):
    degrees = spectral.shape[0]
    block = degrees // 2
    return pl.pallas_call(
        pack_kernel,
        out_shape=jax.ShapeDtypeStruct((CHIPS, 2, degrees, 896), BF16),
        grid=(2,),
        in_specs=[
            pl.BlockSpec((block, 48, 192), lambda i: (i, 0, 0)),
            pl.BlockSpec((block, 192, 192), lambda i: (i, 0, 0)),
            pl.BlockSpec((8, block, 256), lambda i: (0, i, 0)),
        ],
        out_specs=pl.BlockSpec((CHIPS, 2, block, 896), lambda i: (0, 0, i, 0)),
        scratch_shapes=[pltpu.VMEM((6, block * 8, 192), F32)],
        name="pack",
    )(spectral, inverse, legendre)


def contract_kernel(x_ref, valid_ref, place_ref, keep_ref, send_ref):
    for o in range(2):
        x = x_ref[:, o].reshape(256, 896)
        table = jnp.where(valid_ref[:, o : o + 1] > 0, x[:, :256], jnp.zeros((), BF16))
        values = dot(x[:, 256:], place_ref[...], (1, 0)).astype(BF16)
        partial = dot(table, values, (0, 0))
        keep_ref[o] = partial[:, :384]
        send_ref[o] = partial[:, 384:].astype(BF16)


def contract(received, valid, place):
    return pl.pallas_call(
        contract_kernel,
        out_shape=(
            jax.ShapeDtypeStruct((2, 256, 384), F32),
            jax.ShapeDtypeStruct((2, 256, 384), BF16),
        ),
        name="contract",
    )(received, valid, place)


def join_kernel(keep_ref, other_ref, out_ref):
    total = [(keep_ref[o] + other_ref[o].astype(F32)).astype(BF16).astype(F32) for o in range(2)]
    r, c = iota((64, 64), 0), iota((64, 64), 1)
    weave = (c == r % 2 * 32 + r // 2).astype(BF16)
    for ym in range(YM):
        halves = []
        for o in range(2):
            parts = [total[o][t * 32 : (t + 1) * 32, ym * 72 : (ym + 1) * 72] for t in range(8)]
            parts.append(jnp.zeros((32, 64), F32))
            halves.append(jnp.concatenate(parts, axis=1))
        pair = jnp.concatenate(halves, axis=0).astype(BF16)
        out_ref[ym * 64 : (ym + 1) * 64, :] = dot(weave, pair, (1, 0)).astype(BF16)


def join(keep, other):
    return pl.pallas_call(
        join_kernel, out_shape=jax.ShapeDtypeStruct((256, 640), BF16), name="join"
    )(keep, other)


def finish_kernel(x_ref, pick_ref, cos_ref, sin_ref, vort_ref, out_ref, lat_ref):
    @pl.when(pl.program_id(0) == 0)
    def _():
        for k in range(2):
            lat_ref[k] = dot(pick_ref[k], x_ref[...], (1, 1)).astype(BF16)

    flow = dot(lat_ref[0], cos_ref[...], (1, 0)) + dot(lat_ref[1], sin_ref[...], (1, 0))
    u = [flow[c * 96 : (c + 1) * 96] for c in range(3)]
    w = [vort_ref[c].astype(F32) for c in range(3)]
    for c in range(3):
        a, b = (c + 1) % 3, (c + 2) % 3
        out_ref[c] = (u[a] * w[b] - u[b] * w[a]).astype(BF16)


def finish(rows, pick, cos, sin, vorticity):
    width = 512
    return pl.pallas_call(
        finish_kernel,
        out_shape=jax.ShapeDtypeStruct(vorticity.shape, BF16),
        grid=(vorticity.shape[2] // width,),
        in_specs=[
            pl.BlockSpec((256, 640), lambda i: (0, 0)),
            pl.BlockSpec((2, 288, 640), lambda i: (0, 0, 0)),
            pl.BlockSpec((256, width), lambda i: (0, i)),
            pl.BlockSpec((256, width), lambda i: (0, i)),
            pl.BlockSpec((3, 96, width), lambda i: (0, 0, i)),
        ],
        out_specs=pl.BlockSpec((3, 96, width), lambda i: (0, 0, i)),
        scratch_shapes=[pltpu.VMEM((2, 288, 256), BF16)],
        name="finish",
    )(rows, pick, cos, sin, vorticity)


def shards(spectral, inverse, legendre, vorticity, degree_list, order_map):
    ym, core, mem = lax.axis_index("ym"), lax.axis_index("core"), lax.axis_index("mem")
    degrees = spectral.shape[0]
    packed = pack(
        spectral.reshape(degrees, 48, 192), inverse, jnp.transpose(legendre, (0, 2, 1))
    )
    received = lax.all_to_all(packed, ("ys", "ym"), 0, 0, tiled=True)

    orders = lax.dynamic_slice_in_dim(order_map, mem * 8 + ym * 2, 2)
    own = lax.dynamic_index_in_dim(degree_list.reshape(CHIPS, CORES, degrees), core, 1, False)
    valid = (own.reshape(-1)[:, None] >= orders[None, :]).astype(F32)
    col = jnp.arange(640, dtype=jnp.int32)
    ck, s = col // 96, col % 96
    side = jnp.where(s // 12 % 2 == core, 0, 384)
    target = jnp.where(col < 576, side + s // 24 * 72 + ck * 12 + s % 12, -1)
    keep, send = contract(received, valid, one_hot_rows(target, 768))

    other = lax.ppermute(send, "core", [(0, 1), (1, 0)])
    joined = join(keep, other)
    rows = lax.all_to_all(joined.reshape(128, 2, 640), ("ym", "mem"), 0, 0, tiled=True)

    row = jnp.arange(288, dtype=jnp.int32)
    base = row % 8 * 72 + row // 96 * 24 + row // 8 % 12
    pick = jnp.stack([one_hot_rows(base, 640), one_hot_rows(base + 12, 640)])
    member_orders = jnp.transpose(order_map.reshape(32, YM, 2), (1, 0, 2)).reshape(-1)
    cos, sin = trig_tables(member_orders, vorticity.shape[3])
    field = jnp.transpose(vorticity, (0, 2, 1, 3)).reshape(3, 96, vorticity.shape[3])
    out = finish(rows.reshape(256, 640), pick, cos, sin, field)
    return jnp.transpose(out.reshape(3, 12, 8, vorticity.shape[3]), (0, 2, 1, 3))


def solution(mesh):
    fine = Mesh(mesh.devices.reshape(YS, YM, CORES, 32), ("ys", "ym", "core", "mem"))
    grp = ("ys", "ym", "core")
    return jax.shard_map(
        shards,
        mesh=fine,
        in_specs=(
            P(grp, None, None, "mem", None),
            P(grp, None, None),
            P("mem", None, grp),
            P(None, "mem", grp, None),
            P(),
            P(),
        ),
        out_specs=P(None, "mem", grp, None),
        check_vma=False,
    )
```

time: 123 us -> 87.5 us (0.71)
  local copies, waits for them, and re-layouts: 39 us -> 4.99 us
  Pallas kernels: 0 us -> 15.1 us
  between operations: 13.5 us -> 0.08 us
  matrix products: 7.9 us -> 0 us
  starting transfers between devices: 21.7 us -> 27 us
    pallas_call x0 -> x4, Pallas kernels: none -> 15.1 us  [the longest x1 4.7 us: finish(): pl.pallas_call(finish_kernel, out_shape=jax.ShapeDtypeStruct(vorticity.sh...]
    all_to_all x2 -> x0, local copies, waits for them, and re-layouts: 12.8 us -> none  [the longest x1 8.4 us: shards(): lax.all_to_all(latitudinal, 'mem', split_axis=1, concat_axis=0, tiled=True)]
    reshape x2 -> x5, local copies, waits for them, and re-layouts: 11.8 us -> 3.05 us  [the longest x1 1.82 us: shards(): joined.reshape(128, 2, 640)]
    convert_element_type x1 -> x3, other arithmetic: 1.82 us -> 9.83 us  [the longest x1 7.9 us: trig_tables(): (-weight * jnp.sin(angle)).astype(BF16)]
    dot_general x3 -> x0, matrix products: 7.9 us -> none  [the longest x1 3.11 us: solve_radial(): lax.dot_general(rows, flat_profiles, (((2,), (2,)), ((0,), (0,))), prefer...]
    another operation x3 -> x1, other arithmetic: 8.73 us -> 0.98 us  [shards(): pick = jnp.stack([one_hot_rows(base, 640), one_hot_rows(base + 12, 640)])]
    unnamed x12 -> x8, local copies, waits for them, and re-layouts: 8.73 us -> 1.76 us
    ppermute x0 -> x1, starting transfers between devices: none -> 4.47 us  [shards(): other = lax.ppermute(send, 'core', [(0, 1), (1, 0)])]
  transfers between devices with their start and end apart: 3 -> 3, of which waited for: 2 -> 3; matrix products, arithmetic and copies ran while one was open for 27% -> 13% of each run, Pallas kernels for 0% -> 0%
where the time goes in v1:
time: 87.5 us; the launch traced here: 87.1 us
  waiting for transfers between devices  28.8 us (33%)
  starting transfers between devices  27 us (31%)
  Pallas kernels  15.1 us (17%)
  other arithmetic  11.2 us (13%)
  local copies, waits for them, and re-layouts  4.99 us (6%)
    all_to_all x1, waiting for transfers between devices, shards(): received = lax.all_to_all(packed, ('ys', 'ym'), 0, 0, tiled=True)  22.1 us
    all_to_all x1, starting transfers between devices, shards(): lax.all_to_all(joined.reshape(128, 2, 640), ('ym', 'mem'), 0, 0, tiled=True)  14.7 us
    convert_element_type x1, other arithmetic, trig_tables(): (-weight * jnp.sin(angle)).astype(BF16)  7.9 us
    all_to_all x1, starting transfers between devices, shards(): received = lax.all_to_all(packed, ('ys', 'ym'), 0, 0, tiled=True)  7.77 us
    all_to_all x1, waiting for transfers between devices, shards(): lax.all_to_all(joined.reshape(128, 2, 640), ('ym', 'mem'), 0, 0, tiled=True)  5.85 us
    pallas_call x1, Pallas kernels, finish(): pl.pallas_call(finish_kernel, out_shape=jax.ShapeDtypeStruct(vorticity.sh...  4.7 us
    ppermute x1, starting transfers between devices, shards(): other = lax.ppermute(send, 'core', [(0, 1), (1, 0)])  4.47 us
    pallas_call x1, Pallas kernels, pack(): pl.pallas_call(pack_kernel, out_shape=jax.ShapeDtypeStruct((CHIPS, 2, deg...  4.26 us
  transfers between devices with their start and end apart: 3, of which 3 were waited for; matrix products, arithmetic and copies ran while one was open for 13% of the time, Pallas kernels for 0%

profile of v1, /device:TPU:1, one launch (start us, length us, event | category | flops | bytes accessed | tf_op | source)
XLA Modules:
  0.0 87.1 jit_solution(255255275290262727)
XLA Ops:
  0.0 4.3 %pack.1 = bf16[8,2,32,896]{3,2,1,0:T(8,128)(2,1)} custom-call(bf16[32,48,192]{2,1,0:T(8,128)(2,1)} %bitcast.10, bf16[32,192,192]{2,1,0:T(8,128)(2,1)} %inv_ref.1, bf16[8,32,256]{2,1,0:T(8,128)(2,1)} %bitcast.12), custom_call_target="tpu_custom_call" | custom-call | tf_op jit(solution)/shard_map/pack/pallas_call | solution.py:68
  4.3 0.0 copy-start.2
  4.3 0.0 copy-start.3
  4.3 7.8 %all-to-all-start = ((bf16[8,2,32,896]{3,2,1,0:T(8,128)(2,1)}), bf16[8,2,32,896]{3,2,1,0:T(8,128)(2,1)S(1)}, u32[]{:S(2)}, u32[]{:S(2)}) async-start(bf16[8,2,32,896]{3,2,1,0:T(8,128)(2,1)} %pack.1), calls=%async_computation | async-start | bytes 1835008 | tf_op jit(solution)/shard_map/all_to_all | solution.py:163
  12.0 0.0 copy-done.2
  12.0 0.1 reshape.201
  12.1 0.1 ge.15
  12.2 0.0 copy-done.3
  12.2 0.1 dynamic_slice.8
  12.3 0.8 compare_convert_fusion.valid_ref
  13.1 1.2 %fusion.place_ref = bf16[640,768]{1,0:T(8,128)(2,1)} fusion(s32[640]{0:T(1024)S(1)} %fusion.13), kind=kLoop, calls=%fused_computation.2 | loop fusion | flops 983040 | bytes 985600 | tf_op jit(solution)/shard_map/convert_element_type | solution.py:29
  14.3 22.1 %all-to-all-done.x_ref = bf16[8,2,32,896]{3,2,1,0:T(8,128)(2,1)S(1)} async-done(((bf16[8,2,32,896]{3,2,1,0:T(8,128)(2,1)}), bf16[8,2,32,896]{3,2,1,0:T(8,128)(2,1)S(1)}, u32[]{:S(2)}, u32[]{:S(2)}) %all-to-all-start) | async-done | bytes 917536 | tf_op jit(solution)/shard_map/all_to_all | solution.py:163
  36.3 0.0 copy-start
  36.3 1.0 %copy-done = bf16[8,2,32,896]{3,2,1,0:T(8,128)(2,1)} copy-done((bf16[8,2,32,896]{3,2,1,0:T(8,128)(2,1)}, bf16[8,2,32,896]{3,2,1,0:T(8,128)(2,1)S(1)}, u32[]{:S(2)}) %copy-start) | copy-done | bytes 917528
  37.3 3.7 %contract.1 = (f32[2,256,384]{2,1,0:T(8,128)}, bf16[2,256,384]{2,1,0:T(8,128)(2,1)}) custom-call(bf16[8,2,32,896]{3,2,1,0:T(8,128)(2,1)} %copy-done, f32[256,2]{1,0:T(8,128)} %compare_convert_fusion.valid_ref, bf16[640,768]{1,0:T(8,128)(2,1)} %fusion.place_ref), custom_call_target="tpu_custom_call" | custom-call | tf_op jit(solution)/shard_map/contract/pallas_call | solution.py:94
  41.1 4.5 %collective-permute-start = (bf16[2,256,384]{2,1,0:T(8,128)(2,1)}, bf16[2,256,384]{2,1,0:T(8,128)(2,1)S(1)}, u32[]{:S(2)}, u32[]{:S(2)}) collective-permute-start(bf16[2,256,384]{2,1,0:T(8,128)(2,1)} %get-tuple-element.8), channel_id=1, source_target_pairs={{0,32},{32,0},{1,33},{33,1},{2,34},{34,2},{3,35},{35,3},{4,36},{36... | collective-permute-start | bytes 1179656 | tf_op jit(solution)/shard_map/ppermute | solution.py:174
  45.6 0.2 reshape.204
  45.8 0.1 reshape.205
  45.9 0.3 iota_compare_fusion.1
  46.2 0.9 %collective-permute-done.other_ref = bf16[2,256,384]{2,1,0:T(8,128)(2,1)S(1)} collective-permute-done((bf16[2,256,384]{2,1,0:T(8,128)(2,1)}, bf16[2,256,384]{2,1,0:T(8,128)(2,1)S(1)}, u32[]{:S(2)}, u32[]{:S(2)}) %collective-permute-start) | collective-permute-done | bytes 393248 | tf_op jit(solution)/shard_map/ppermute | solution.py:174
  47.1 0.0 copy-start.1
  47.1 0.7 copy-done.1
  47.8 2.4 %join.1 = bf16[256,640]{1,0:T(8,128)(2,1)} custom-call(f32[2,256,384]{2,1,0:T(8,128)} %get-tuple-element.7.keep_ref, bf16[2,256,384]{2,1,0:T(8,128)(2,1)} %copy-done.1), custom_call_target="tpu_custom_call" | custom-call | tf_op jit(solution)/shard_map/join/pallas_call | solution.py:119
  50.2 1.8 %reshape.202 = bf16[128,2,640]{2,1,0:T(2,128)(2,1)} reshape(bf16[256,640]{1,0:T(8,128)(2,1)} %join.1) | data formatting | bytes 655360 | tf_op jit(solution)/shard_map/reshape | solution.py:176
  52.0 14.7 %all-to-all-start.1 = ((bf16[128,2,640]{2,1,0:T(2,128)(2,1)}), bf16[128,2,640]{2,1,0:T(2,128)(2,1)S(1)}, u32[]{:S(2)}, u32[]{:S(2)}) async-start(bf16[128,2,640]{2,1,0:T(2,128)(2,1)} %reshape.202), calls=%async_computation.1 | async-start | bytes 655360 | tf_op jit(solution)/shard_map/all_to_all | solution.py:176
  66.8 1.0 %add_convert_fusion.pick_ref = bf16[2,288,640]{2,1,0:T(8,128)(2,1)} fusion(pred[1,288,640]{2,1,0:T(8,128)(4,1)S(1)} %get-tuple-element.13, pred[1,288,640]{2,1,0:T(8,128)(4,1)S(1)} %get-tuple-element.14), kind=kLoop, calls=%fused_computation.11 | loop fusion | flops 737280 | bytes 1105920 | tf_op jit(solution)/shard_map/stack | solution.py:180
  67.8 7.9 %multiply_convert_fusion = (bf16[256,1536]{1,0:T(8,128)(2,1)}, bf16[256,1536]{1,0:T(8,128)(2,1)}) fusion(f32[256]{0:T(256)S(1)} %get-tuple-element.11, s32[256]{0:T(256)S(1)} %reshape.205, f32[256]{0:T(256)S(1)} %get-tuple-element.12), kind=kLoop, calls=%fused_computation.5 | loop fusion | flops 5111808 | bytes 1575936 | tf_op jit(solution)/shard_map/convert_element_type | solution.py:25
  75.7 5.8 %all-to-all-done.1 = bf16[128,2,640]{2,1,0:T(2,128)(2,1)S(1)} async-done(((bf16[128,2,640]{2,1,0:T(2,128)(2,1)}), bf16[128,2,640]{2,1,0:T(2,128)(2,1)S(1)}, u32[]{:S(2)}, u32[]{:S(2)}) %all-to-all-start.1) | async-done | bytes 327712 | tf_op jit(solution)/shard_map/all_to_all | solution.py:176
  81.5 0.8 reshape.203.x_ref
  82.4 4.7 %finish.1 = bf16[3,96,1536]{2,1,0:T(8,128)(2,1)} custom-call(bf16[256,640]{1,0:T(8,128)(2,1)} %reshape.203.x_ref, bf16[2,288,640]{2,1,0:T(8,128)(2,1)} %add_convert_fusion.pick_ref, bf16[256,1536]{1,0:T(8,128)(2,1)} %get-tuple-element.10.cos_ref, bf16[256,1536]{1,0:T(8,128)(2,1)} %get-tuple-element.9.sin_ref, bf16[3,96,1536]{2,1,0:T(8,128)(2,1)} %bitcast.9), custom_call_target="tpu_custom_call" | custom-call | tf_op jit(solution)/shard_map/finish/pallas_call | solution.py:140
  (6 shorter events, 0.1 us)
Async XLA Ops:
  4.3 7.8 %copy-start.2 = (s32[512]{0:T(512)S(1)}, s32[512]{0:T(512)}, u32[]{:S(2)}) copy-start(s32[512]{0:T(512)} %param.10) | copy-start | bytes 6148
  4.3 8.0 %copy-start.3 = (s32[256]{0:T(256)S(1)}, s32[256]{0:T(256)}, u32[]{:S(2)}) copy-start(s32[256]{0:T(256)} %param.11) | copy-start | bytes 3076
  4.3 32.1 %all-to-all-start = ((bf16[8,2,32,896]{3,2,1,0:T(8,128)(2,1)}), bf16[8,2,32,896]{3,2,1,0:T(8,128)(2,1)S(1)}, u32[]{:S(2)}, u32[]{:S(2)}) async-start(bf16[8,2,32,896]{3,2,1,0:T(8,128)(2,1)} %pack.1), calls=%async_computation | async-start | bytes 1835008 | tf_op jit(solution)/shard_map/all_to_all | solution.py:163
  36.3 1.0 %copy-start = (bf16[8,2,32,896]{3,2,1,0:T(8,128)(2,1)}, bf16[8,2,32,896]{3,2,1,0:T(8,128)(2,1)S(1)}, u32[]{:S(2)}) copy-start(bf16[8,2,32,896]{3,2,1,0:T(8,128)(2,1)S(1)} %all-to-all-done.x_ref) | copy-start | bytes 2752516
  41.1 6.0 %collective-permute-start = (bf16[2,256,384]{2,1,0:T(8,128)(2,1)}, bf16[2,256,384]{2,1,0:T(8,128)(2,1)S(1)}, u32[]{:S(2)}, u32[]{:S(2)}) collective-permute-start(bf16[2,256,384]{2,1,0:T(8,128)(2,1)} %get-tuple-element.8), channel_id=1, source_target_pairs={{0,32},{32,0},{1,33},{33,1},{2,34},{34,2},{3,35},{35,3},{4,36},{36... | collective-permute-start | bytes 1179656 | tf_op jit(solution)/shard_map/ppermute | solution.py:174
  47.1 0.7 copy-start.1
  52.0 29.5 %all-to-all-start.1 = ((bf16[128,2,640]{2,1,0:T(2,128)(2,1)}), bf16[128,2,640]{2,1,0:T(2,128)(2,1)S(1)}, u32[]{:S(2)}, u32[]{:S(2)}) async-start(bf16[128,2,640]{2,1,0:T(2,128)(2,1)} %reshape.202), calls=%async_computation.1 | async-start | bytes 655360 | tf_op jit(solution)/shard_map/all_to_all | solution.py:176

commit v2 on v1

v2 whole, which is shorter than its diff:
```python
import math

import jax
import jax.numpy as jnp
from jax import lax
from jax.experimental import pallas as pl
from jax.experimental.pallas import tpu as pltpu
from jax.sharding import Mesh
from jax.sharding import PartitionSpec as P

YS, YM, CORES = 2, 4, 2
CHIPS = YS * YM
F32, BF16 = jnp.float32, jnp.bfloat16
STEPS = 4
PARAMS = pltpu.CompilerParams(vmem_limit_bytes=16 << 20)


def dot(left, right, contract):
    return lax.dot_general(left, right, ((contract[:1], contract[1:]), ((), ())), preferred_element_type=F32)


def iota(shape, axis):
    return lax.broadcasted_iota(jnp.int32, shape, axis)


def pack_kernel(spec_hbm, inv_hbm, leg_hbm, out_ref, spec_ref, inv_ref, leg_ref, solved_ref, sems):
    degrees = spec_ref.shape[0]
    rows = degrees * 8
    step = degrees // STEPS
    copies = []
    for i in range(STEPS):
        cut = pl.ds(i * step, step)
        copies.append(pltpu.make_async_copy(inv_hbm.at[cut], inv_ref.at[cut], sems.at[2 * i]))
        copies.append(pltpu.make_async_copy(spec_hbm.at[cut], spec_ref.at[cut], sems.at[2 * i + 1]))
    copies.append(pltpu.make_async_copy(leg_hbm, leg_ref, sems.at[2 * STEPS]))
    for copy in copies:
        copy.start()
    for i in range(STEPS):
        copies[2 * i].wait()
        copies[2 * i + 1].wait()
        for l in range(i * step, (i + 1) * step):
            product = dot(spec_ref[l], inv_ref[l], (1, 1))
            for ck in range(6):
                solved_ref[ck, l * 8 : (l + 1) * 8, :] = product[ck * 8 : (ck + 1) * 8, :]
    copies[-1].wait()
    r, c = iota((256, 256), 0), iota((256, 256), 1)
    turn = (r == c % 32 * 8 + c // 32).astype(BF16)
    table = dot(leg_ref[...].reshape(256, 256), turn, (1, 0)).astype(BF16)
    for chip in range(CHIPS):
        for o in range(2):
            at = (chip % YM * 2 + o) * degrees
            out_ref[chip, :, o * 256 : (o + 1) * 256] = table[at : at + degrees, :]
    r, c = iota((rows, rows), 0), iota((rows, rows), 1)
    swap = (c == r % degrees * 8 + r // degrees).astype(BF16)
    by_order = [dot(swap, solved_ref[ck].astype(BF16), (1, 0)) for ck in range(6)]
    half = by_order[0].shape[1] // YS
    for ys in range(YS):
        for ym in range(YM):
            parts = []
            for o in range(2):
                at = (ym * 2 + o) * degrees
                parts += [v[at : at + degrees, ys * half : (ys + 1) * half] for v in by_order]
            out_ref[ys * YM + ym, :, 512:] = jnp.concatenate(parts, axis=1).astype(BF16)


def pack(spectral, inverse, legendre):
    degrees = spectral.shape[0]
    return pl.pallas_call(
        pack_kernel,
        out_shape=jax.ShapeDtypeStruct((CHIPS, degrees, 1664), BF16),
        in_specs=[pl.BlockSpec(memory_space=pl.ANY)] * 3,
        scratch_shapes=[
            pltpu.VMEM(spectral.shape, BF16),
            pltpu.VMEM(inverse.shape, BF16),
            pltpu.VMEM(legendre.shape, BF16),
            pltpu.VMEM((6, degrees * 8, 192), F32),
            pltpu.SemaphoreType.DMA((2 * STEPS + 1,)),
        ],
        compiler_params=pltpu.CompilerParams(vmem_limit_bytes=60 << 20),
        name="pack",
    )(spectral, inverse, legendre)


def turned(values, index):
    hit = iota(index.shape, 1) == index
    return jnp.sum(jnp.where(hit, values, 0), axis=1, keepdims=True)


def tables_kernel(where_ref, order_ref, degree_ref, info_ref, place_ref, pick_ref, cos_ref, sin_ref):
    core, first = where_ref[0], where_ref[1]
    r = iota((256, 512), 0)
    own = turned(degree_ref[...].astype(F32), r // 32 * 64 + core * 32 + r % 32)
    orders = order_ref[...].astype(F32)
    for o in range(2):
        order = turned(orders, jnp.full((256, 256), first + o, jnp.int32))
        info_ref[:, o : o + 1] = (own >= order).astype(F32)
    q, col = iota((640, 768), 0), iota((640, 768), 1)
    ck, s = q // 96, q % 96
    side = jnp.where(s // 12 % 2 == core, 0, 384)
    hit = (col == side + s // 24 * 72 + ck * 12 + s % 12) & (q < 576)
    place_ref[...] = hit.astype(F32).astype(BF16)
    row, col = iota((288, 640), 0), iota((288, 640), 1)
    hit = col == row % 8 * 72 + row // 96 * 24 + row // 8 % 12
    pick_ref[...] = hit.astype(F32).astype(BF16)
    r = iota((256, 256), 0)
    order = turned(orders, r % 64 // 2 * 8 + r // 64 * 2 + r % 2)
    weight = jnp.where(order == 0, 1.0, 2.0)
    info_ref[:, 2:3] = 1.0 - 2.0 * (order - 2.0 * jnp.floor(order * 0.5))
    half = cos_ref.shape[1]
    count = 2 * half
    for at in range(0, half, 128):
        product = order * (iota((256, 128), 1) + at).astype(F32)
        phase = product - jnp.floor(product * (1.0 / count)) * count
        phase = jnp.where(phase < 0, phase + count, phase)
        phase = jnp.where(phase >= count, phase - count, phase)
        angle = phase * (2.0 * math.pi / count)
        cos_ref[:, at : at + 128] = (weight * jnp.cos(angle)).astype(BF16)
        sin_ref[:, at : at + 128] = (-weight * jnp.sin(angle)).astype(BF16)


def tables(where, order_map, degree_list, count):
    return pl.pallas_call(
        tables_kernel,
        out_shape=(
            jax.ShapeDtypeStruct((256, 3), F32),
            jax.ShapeDtypeStruct((640, 768), BF16),
            jax.ShapeDtypeStruct((288, 640), BF16),
            jax.ShapeDtypeStruct((256, count // 2), BF16),
            jax.ShapeDtypeStruct((256, count // 2), BF16),
        ),
        in_specs=[pl.BlockSpec(memory_space=pltpu.SMEM)]
        + [pl.BlockSpec(memory_space=pltpu.VMEM)] * 2,
        compiler_params=PARAMS,
        name="tables",
    )(where, order_map[None, :], degree_list[None, :])


def contract_kernel(x_ref, info_ref, place_ref, keep_ref, send_ref):
    for o in range(2):
        table = x_ref[:, :, o * 256 : (o + 1) * 256].reshape(256, 256)
        table = jnp.where(info_ref[:, o : o + 1] > 0, table, jnp.zeros((), BF16))
        radial = x_ref[:, :, 512 + o * 512 : 1152 + o * 512].reshape(256, 640)
        if o:
            radial = jnp.concatenate([radial[:, 64:], radial[:, :64]], axis=1)
        values = dot(radial, place_ref[...], (1, 0)).astype(BF16)
        partial = dot(table, values, (0, 0))
        keep_ref[o] = partial[:, :384]
        send_ref[o] = partial[:, 384:].astype(BF16)


def contract(received, info, place):
    return pl.pallas_call(
        contract_kernel,
        out_shape=(
            jax.ShapeDtypeStruct((2, 256, 384), F32),
            jax.ShapeDtypeStruct((2, 256, 384), BF16),
        ),
        compiler_params=PARAMS,
        name="contract",
    )(received, info, place)


def join_kernel(keep_ref, other_ref, out_ref):
    total = [(keep_ref[o] + other_ref[o].astype(F32)).astype(BF16).astype(F32) for o in range(2)]
    r, c = iota((64, 64), 0), iota((64, 64), 1)
    weave = (c == r % 2 * 32 + r // 2).astype(BF16)
    for ym in range(YM):
        halves = []
        for o in range(2):
            parts = [total[o][t * 32 : (t + 1) * 32, ym * 72 : (ym + 1) * 72] for t in range(8)]
            parts.append(jnp.zeros((32, 64), F32))
            halves.append(jnp.concatenate(parts, axis=1))
        pair = jnp.concatenate(halves, axis=0).astype(BF16)
        out_ref[ym * 64 : (ym + 1) * 64, :] = dot(weave, pair, (1, 0)).astype(BF16)


def join(keep, other):
    return pl.pallas_call(
        join_kernel,
        out_shape=jax.ShapeDtypeStruct((256, 640), BF16),
        compiler_params=PARAMS,
        name="join",
    )(keep, other)


def finish_kernel(x_ref, info_ref, pick_ref, cos_ref, sin_ref, vort_ref, out_ref, lat_ref):
    step = pl.program_id(0)
    side = step // (pl.num_programs(0) // 2)

    @pl.when(step == 0)
    def _():
        x = x_ref[...].astype(F32)
        x = jnp.concatenate([x, x * info_ref[:, 2:3]], axis=0)
        for k in range(2):
            turned_x = jnp.concatenate([x[:, 12:], x[:, :12]], axis=1) if k else x
            rows = dot(pick_ref[...], turned_x.astype(BF16), (1, 1)).astype(BF16)
            for h in range(2):
                lat_ref[h, k] = rows[:, h * 256 : (h + 1) * 256]

    flow = dot(lat_ref[side, 0], cos_ref[...], (1, 0)) + dot(lat_ref[side, 1], sin_ref[...], (1, 0))
    u = [flow[c * 96 : (c + 1) * 96] for c in range(3)]
    w = [vort_ref[c].astype(F32) for c in range(3)]
    for c in range(3):
        a, b = (c + 1) % 3, (c + 2) % 3
        out_ref[c] = (u[a] * w[b] - u[b] * w[a]).astype(BF16)


def finish(rows, info, pick, cos, sin, vorticity):
    width = 384
    blocks = cos.shape[1] // width
    return pl.pallas_call(
        finish_kernel,
        out_shape=jax.ShapeDtypeStruct(vorticity.shape, BF16),
        grid=(2 * blocks,),
        in_specs=[
            pl.BlockSpec((256, 640), lambda i: (0, 0)),
            pl.BlockSpec((256, 3), lambda i: (0, 0)),
            pl.BlockSpec((288, 640), lambda i: (0, 0)),
            pl.BlockSpec((256, width), lambda i: (0, i % blocks)),
            pl.BlockSpec((256, width), lambda i: (0, i % blocks)),
            pl.BlockSpec((3, 96, width), lambda i: (0, 0, i)),
        ],
        out_specs=pl.BlockSpec((3, 96, width), lambda i: (0, 0, i)),
        scratch_shapes=[pltpu.VMEM((2, 2, 288, 256), BF16)],
        compiler_params=PARAMS,
        name="finish",
    )(rows, info, pick, cos, sin, vorticity)


def shards(spectral, inverse, legendre, vorticity, degree_list, order_map):
    ym, core, mem = lax.axis_index("ym"), lax.axis_index("core"), lax.axis_index("mem")
    degrees = spectral.shape[0]
    packed = pack(
        spectral.reshape(degrees, 48, 192), inverse, jnp.transpose(legendre, (0, 2, 1))
    )
    received = lax.all_to_all(packed, ("ys", "ym"), 0, 0, tiled=True)
    where = jnp.stack([core, mem * 8 + ym * 2]).astype(jnp.int32)
    count = vorticity.shape[3]
    info, place, pick, cos, sin = tables(where, order_map, degree_list, count)
    keep, send = contract(received, info, place)
    other = lax.ppermute(send, "core", [(0, 1), (1, 0)])
    joined = join(keep, other)
    rows = lax.all_to_all(joined.reshape(128, 2, 640), ("ym", "mem"), 0, 0, tiled=True)

    field = jnp.transpose(vorticity, (0, 2, 1, 3)).reshape(3, 96, count)
    out = finish(rows.reshape(256, 640), info, pick, cos, sin, field)
    return jnp.transpose(out.reshape(3, 12, 8, count), (0, 2, 1, 3))


def solution(mesh):
    fine = Mesh(mesh.devices.reshape(YS, YM, CORES, 32), ("ys", "ym", "core", "mem"))
    grp = ("ys", "ym", "core")
    return jax.shard_map(
        shards,
        mesh=fine,
        in_specs=(
            P(grp, None, None, "mem", None),
            P(grp, None, None),
            P("mem", None, grp),
            P(None, "mem", grp, None),
            P(),
            P(),
        ),
        out_specs=P(None, "mem", grp, None),
        check_vma=False,
    )
```

time: 87.5 us -> 75.6 us (0.86)
  blocking collectives: 0 us -> 29.2 us
  starting transfers between devices: 27 us -> 12.3 us
  waiting for transfers between devices: 28.8 us -> 17.2 us
  other arithmetic: 11.2 us -> 0.08 us
  local copies, waits for them, and re-layouts: 4.99 us -> 1.74 us
    all_to_all x0 -> x1, blocking collectives: none -> 29.2 us  [shards(): lax.all_to_all(joined.reshape(128, 2, 640), ('ym', 'mem'), 0, 0, tiled=True)]
    all_to_all x1 -> x0, starting transfers between devices: 14.7 us -> none  [shards(): lax.all_to_all(joined.reshape(128, 2, 640), ('ym', 'mem'), 0, 0, tiled=True)]
    convert_element_type x3 -> x0, other arithmetic: 9.83 us -> none  [the longest x1 7.9 us: trig_tables(): (-weight * jnp.sin(angle)).astype(BF16)]
    all_to_all x1, waiting for transfers between devices: 22.1 us -> 15.8 us  [shards(): received = lax.all_to_all(packed, ('ys', 'ym'), 0, 0, tiled=True)]
    all_to_all x1 -> x0, waiting for transfers between devices: 5.85 us -> none  [shards(): lax.all_to_all(joined.reshape(128, 2, 640), ('ym', 'mem'), 0, 0, tiled=True)]
    pallas_call x1 -> x2, Pallas kernels: 4.26 us -> 9.64 us  [the longest x1 5.5 us: tables(): pl.pallas_call(tables_kernel, out_shape=(jax.ShapeDtypeStruct((256, 3), F...]
    pallas_call x1, Pallas kernels: 3.74 us -> 1.23 us  [contract(): pl.pallas_call(contract_kernel, out_shape=(jax.ShapeDtypeStruct((2, 256,...]
    pallas_call x1, Pallas kernels: 2.37 us -> 0.4 us  [join(): pl.pallas_call(join_kernel, out_shape=jax.ShapeDtypeStruct((256, 640), BF...]
  transfers between devices with their start and end apart: 3 -> 2, of which waited for: 3 -> 2; matrix products, arithmetic and copies ran while one was open for 13% -> 0% of each run, Pallas kernels for 0% -> 7%
where the time goes in v2:
time: 75.6 us; the launch traced here: 75.4 us
  blocking collectives  29.2 us (39%)
  waiting for transfers between devices  17.2 us (23%)
  Pallas kernels  14.7 us (19%)
  starting transfers between devices  12.3 us (16%)
  local copies, waits for them, and re-layouts  1.74 us (2%)
    all_to_all x1, blocking collectives, shards(): lax.all_to_all(joined.reshape(128, 2, 640), ('ym', 'mem'), 0, 0, tiled=True)  29.2 us
    all_to_all x1, waiting for transfers between devices, shards(): received = lax.all_to_all(packed, ('ys', 'ym'), 0, 0, tiled=True)  15.8 us
    all_to_all x1, starting transfers between devices, shards(): received = lax.all_to_all(packed, ('ys', 'ym'), 0, 0, tiled=True)  7.66 us
    pallas_call x1, Pallas kernels, tables(): pl.pallas_call(tables_kernel, out_shape=(jax.ShapeDtypeStruct((256, 3), F...  5.5 us
    ppermute x1, starting transfers between devices, shards(): other = lax.ppermute(send, 'core', [(0, 1), (1, 0)])  4.65 us
    pallas_call x1, Pallas kernels, pack(): pl.pallas_call(pack_kernel, out_shape=jax.ShapeDtypeStruct((CHIPS, degree...  4.14 us
    pallas_call x1, Pallas kernels, finish(): pl.pallas_call(finish_kernel, out_shape=jax.ShapeDtypeStruct(vorticity.sh...  3.47 us
  transfers between devices with their start and end apart: 2, of which 2 were waited for; matrix products, arithmetic and copies ran while one was open for 0% of the time, Pallas kernels for 7%

profile of v2, /device:TPU:1, one launch (start us, length us, event | category | flops | bytes accessed | tf_op | source)
XLA Modules:
  0.0 75.4 jit_solution(16329215226641302801)
XLA Ops:
  0.0 0.0 copy-start.5
  0.0 0.0 copy-start.6
  0.0 4.1 %pack.1 = bf16[8,32,1664]{2,1,0:T(8,128)(2,1)} custom-call(bf16[32,48,192]{2,1,0:T(8,128)(2,1)} %bitcast.15, bf16[32,192,192]{2,1,0:T(8,128)(2,1)} %inv_hbm.1, bf16[8,32,256]{2,1,0:T(8,128)(2,1)} %bitcast.16), custom_call_target="tpu_custom_call" | custom-call | tf_op jit(solution)/shard_map/pack/pallas_call | solution.py:68
  4.2 7.7 %all-to-all-start = ((bf16[8,32,1664]{2,1,0:T(8,128)(2,1)}), bf16[8,32,1664]{2,1,0:T(8,128)(2,1)S(1)}, u32[]{:S(2)}, u32[]{:S(2)}) async-start(bf16[8,32,1664]{2,1,0:T(8,128)(2,1)} %pack.1), calls=%async_computation | async-start | bytes 1703936 | tf_op jit(solution)/shard_map/all_to_all | solution.py:236
  11.8 0.0 copy-start
  11.8 0.1 pad_add_fusion.where_ref
  11.9 0.0 copy-done.5
  11.9 0.0 copy-done.6
  11.9 5.5 %tables.1 = (f32[256,3]{1,0:T(8,128)S(1)}, bf16[640,768]{1,0:T(8,128)(2,1)S(1)}, bf16[288,640]{1,0:T(8,128)(2,1)S(1)}, bf16[256,768]{1,0:T(8,128)(2,1)S(1)}, bf16[256,768]{1,0:T(8,128)(2,1)S(1)}) custom-call(s32[2]{0:T(128)S(1)} %pad_add_fusion.where_ref, s32[1,256]{1,0:T(1,128)S(1)} %bitcast.14, s32[1,512]{1,0:T(1,128)S(1)} %bitcast.13), custom_call_target="tpu_custom_call" | custom-call | tf_op jit(solution)/shard_map/tables/pallas_call | solution.py:122
  17.4 0.0 copy-start.1
  17.4 0.7 copy-done.1
  18.2 0.0 copy-start.3
  18.2 0.7 copy-done.3
  18.9 15.8 %all-to-all-done.x_ref = bf16[8,32,1664]{2,1,0:T(8,128)(2,1)S(1)} async-done(((bf16[8,32,1664]{2,1,0:T(8,128)(2,1)}), bf16[8,32,1664]{2,1,0:T(8,128)(2,1)S(1)}, u32[]{:S(2)}, u32[]{:S(2)}) %all-to-all-start) | async-done | bytes 852000 | tf_op jit(solution)/shard_map/all_to_all | solution.py:236
  34.7 1.2 %contract.1 = (f32[2,256,384]{2,1,0:T(8,128)S(1)}, bf16[2,256,384]{2,1,0:T(8,128)(2,1)S(1)}) custom-call(bf16[8,32,1664]{2,1,0:T(8,128)(2,1)S(1)} %all-to-all-done.x_ref, f32[256,3]{1,0:T(8,128)S(1)} %get-tuple-element.12.info_ref, bf16[640,768]{1,0:T(8,128)(2,1)S(1)} %get-tuple-element.13.place_ref), custom_call_target="tpu_custom_call" | custom-call | tf_op jit(solution)/shard_map/contract/pallas_call | solution.py:152
  36.0 0.0 copy-start.2
  36.0 0.0 copy-start.4
  36.0 4.7 %collective-permute-start = (bf16[2,256,384]{2,1,0:T(8,128)(2,1)S(1)}, bf16[2,256,384]{2,1,0:T(8,128)(2,1)S(1)}, u32[]{:S(2)}, u32[]{:S(2)}) collective-permute-start(bf16[2,256,384]{2,1,0:T(8,128)(2,1)S(1)} %get-tuple-element.15), channel_id=1, source_target_pairs={{0,32},{32,0},{1,33},{33,1},{2,34},{34,2},{3,35},{35,3},{4,36},{36... | collective-permute-start | bytes 1179656 | tf_op jit(solution)/shard_map/ppermute | solution.py:241
  40.6 1.3 %collective-permute-done.other_ref = bf16[2,256,384]{2,1,0:T(8,128)(2,1)S(1)} collective-permute-done((bf16[2,256,384]{2,1,0:T(8,128)(2,1)S(1)}, bf16[2,256,384]{2,1,0:T(8,128)(2,1)S(1)}, u32[]{:S(2)}, u32[]{:S(2)}) %collective-permute-start) | collective-permute-done | bytes 393248 | tf_op jit(solution)/shard_map/ppermute | solution.py:241
  42.0 0.4 join.1
  42.4 0.1 reshape.16
  42.5 29.2 %all_to_all.10 = bf16[128,2,640]{2,1,0:T(2,128)(2,1)S(1)} all-to-all(bf16[128,2,640]{2,1,0:T(2,128)(2,1)S(1)} %reshape.16), channel_id=1, replica_groups=mesh['ys'=2,'ym'=4,'core'=2,'mem'=32] {'ym','mem'}, dimensions={0} | all-to-all | bytes 655360 | tf_op jit(solution)/shard_map/all_to_all | solution.py:243
  71.7 0.1 reshape.17.x_ref
  71.9 0.0 copy-done
  71.9 0.0 copy-done.2
  71.9 0.0 copy-done.4
  71.9 3.5 %finish.1 = bf16[3,96,1536]{2,1,0:T(8,128)(2,1)} custom-call(bf16[256,640]{1,0:T(8,128)(2,1)S(1)} %reshape.17.x_ref, f32[256,3]{1,0:T(8,128)S(1)} %get-tuple-element.12.info_ref, bf16[288,640]{1,0:T(8,128)(2,1)S(1)} %copy-done.4, bf16[256,768]{1,0:T(8,128)(2,1)S(1)} %get-tuple-element.17.cos_ref, bf16[256,768]{1,0:T(8,128)(2,1)S(1)} %copy-done.2, ...), custom_call_target="tpu_custom_call" | custom-call | tf_op jit(solution)/shard_map/finish/pallas_call | solution.py:211
Async XLA Ops:
  0.0 11.9 %copy-start.5 = (s32[512]{0:T(512)S(1)}, s32[512]{0:T(512)}, u32[]{:S(2)}) copy-start(s32[512]{0:T(512)} %param.10) | copy-start | bytes 6148
  0.0 11.9 %copy-start.6 = (s32[256]{0:T(256)S(1)}, s32[256]{0:T(256)}, u32[]{:S(2)}) copy-start(s32[256]{0:T(256)} %param.11) | copy-start | bytes 3076
  4.2 30.6 %all-to-all-start = ((bf16[8,32,1664]{2,1,0:T(8,128)(2,1)}), bf16[8,32,1664]{2,1,0:T(8,128)(2,1)S(1)}, u32[]{:S(2)}, u32[]{:S(2)}) async-start(bf16[8,32,1664]{2,1,0:T(8,128)(2,1)} %pack.1), calls=%async_computation | async-start | bytes 1703936 | tf_op jit(solution)/shard_map/all_to_all | solution.py:236
  11.8 60.1 %copy-start = (bf16[3,8,12,1536]{3,1,2,0:T(8,128)(2,1)S(1)}, bf16[3,8,12,1536]{3,1,2,0:T(8,128)(2,1)}, u32[]{:S(2)}) copy-start(bf16[3,8,12,1536]{3,1,2,0:T(8,128)(2,1)} %param.9) | copy-start | bytes 2654212
  17.4 0.7 copy-start.1
  18.2 0.7 copy-start.3
  36.0 35.9 %copy-start.2 = (bf16[256,768]{1,0:T(8,128)(2,1)S(1)}, bf16[256,768]{1,0:T(8,128)(2,1)}, u32[]{:S(2)}) copy-start(bf16[256,768]{1,0:T(8,128)(2,1)} %copy-done.1) | copy-start | bytes 1179652
  36.0 35.9 %copy-start.4 = (bf16[288,640]{1,0:T(8,128)(2,1)S(1)}, bf16[288,640]{1,0:T(8,128)(2,1)}, u32[]{:S(2)}) copy-start(bf16[288,640]{1,0:T(8,128)(2,1)} %copy-done.3) | copy-start | bytes 1105924
  36.0 6.0 %collective-permute-start = (bf16[2,256,384]{2,1,0:T(8,128)(2,1)S(1)}, bf16[2,256,384]{2,1,0:T(8,128)(2,1)S(1)}, u32[]{:S(2)}, u32[]{:S(2)}) collective-permute-start(bf16[2,256,384]{2,1,0:T(8,128)(2,1)S(1)} %get-tuple-element.15), channel_id=1, source_target_pairs={{0,32},{32,0},{1,33},{33,1},{2,34},{34,2},{3,35},{35,3},{4,36},{36... | collective-permute-start | bytes 1179656 | tf_op jit(solution)/shard_map/ppermute | solution.py:241

commit v3 on v2

v3 whole, which is shorter than its diff:
```python
import math

import jax
import jax.numpy as jnp
from jax import lax
from jax.experimental import pallas as pl
from jax.experimental.pallas import tpu as pltpu
from jax.sharding import Mesh
from jax.sharding import PartitionSpec as P

YS, YM, CORES = 2, 4, 2
CHIPS = YS * YM
F32, BF16 = jnp.float32, jnp.bfloat16
STEPS = 4
WIDTH = 256
PARAMS = pltpu.CompilerParams(vmem_limit_bytes=16 << 20)


def dot(left, right, contract):
    return lax.dot_general(left, right, ((contract[:1], contract[1:]), ((), ())), preferred_element_type=F32)


def iota(shape, axis):
    return lax.broadcasted_iota(jnp.int32, shape, axis)


def pack_kernel(
    spec_hbm, inv_hbm, leg_hbm, out_hbm, out_ref, spec_ref, inv_ref, leg_ref, solved_ref, sems, out_sems
):
    degrees = spec_ref.shape[0]
    rows = degrees * 8
    step = degrees // STEPS
    copies = [pltpu.make_async_copy(leg_hbm, leg_ref, sems.at[2 * STEPS])]
    for i in range(STEPS):
        cut = pl.ds(i * step, step)
        copies.append(pltpu.make_async_copy(inv_hbm.at[cut], inv_ref.at[cut], sems.at[2 * i]))
        copies.append(pltpu.make_async_copy(spec_hbm.at[cut], spec_ref.at[cut], sems.at[2 * i + 1]))
    for copy in copies:
        copy.start()
    r, c = iota((256, 256), 0), iota((256, 256), 1)
    turn = (r == c % 32 * 8 + c // 32).astype(BF16)
    swap = (c == r % degrees * 8 + r // degrees).astype(BF16)
    copies[0].wait()
    table = dot(leg_ref[...].reshape(rows, 256), turn, (1, 0)).astype(BF16)
    for chip in range(CHIPS):
        for o in range(2):
            at = (chip % YM * 2 + o) * degrees
            out_ref[chip, :, o * 256 : (o + 1) * 256] = table[at : at + degrees, :]
    for i in range(STEPS):
        copies[2 * i + 1].wait()
        copies[2 * i + 2].wait()
        for l in range(i * step, (i + 1) * step):
            product = dot(spec_ref[l], inv_ref[l], (1, 1))
            for ck in range(6):
                solved_ref[ck, l * 8 : (l + 1) * 8, :] = product[ck * 8 : (ck + 1) * 8, :]
    r, c = iota((192, 192), 0), iota((192, 192), 1)
    side = (r // 12 % 2 != lax.axis_index("core")).astype(jnp.int32)
    near = (c == r // 96 * 96 + side * 48 + r % 96 // 24 * 12 + r % 12).astype(F32).astype(BF16)
    by_order = [dot(swap, solved_ref[ck].astype(BF16), (1, 0)).astype(BF16) for ck in range(6)]
    by_order = [dot(v, near, (1, 0)) for v in by_order]
    half = by_order[0].shape[1] // YS
    sends = []
    for ys in range(YS):
        for ym in range(YM):
            parts = []
            for o in range(2):
                at = (ym * 2 + o) * degrees
                parts += [v[at : at + degrees, ys * half : (ys + 1) * half] for v in by_order]
            chip = ys * YM + ym
            out_ref[chip, :, 512:] = jnp.concatenate(parts, axis=1).astype(BF16)
            sends.append(pltpu.make_async_copy(out_ref.at[chip], out_hbm.at[chip], out_sems.at[chip]))
            sends[-1].start()
    for send in sends:
        send.wait()


def pack(spectral, inverse, legendre):
    degrees = spectral.shape[0]
    return pl.pallas_call(
        pack_kernel,
        out_shape=jax.ShapeDtypeStruct((CHIPS, degrees, 1664), BF16),
        in_specs=[pl.BlockSpec(memory_space=pl.ANY)] * 3,
        out_specs=pl.BlockSpec(memory_space=pl.ANY),
        scratch_shapes=[
            pltpu.VMEM((CHIPS, degrees, 1664), BF16),
            pltpu.VMEM(spectral.shape, BF16),
            pltpu.VMEM(inverse.shape, BF16),
            pltpu.VMEM(legendre.shape, BF16),
            pltpu.VMEM((6, degrees * 8, 192), F32),
            pltpu.SemaphoreType.DMA((2 * STEPS + 1,)),
            pltpu.SemaphoreType.DMA((CHIPS,)),
        ],
        compiler_params=pltpu.CompilerParams(vmem_limit_bytes=60 << 20),
        name="pack",
    )(spectral, inverse, legendre)


def turned(values, index):
    hit = iota(index.shape, 1) == index
    return jnp.sum(jnp.where(hit, values, 0), axis=1, keepdims=True)


def tables_kernel(where_ref, order_ref, degree_ref, info_ref, place_ref, pick_ref, cos_ref, sin_ref):
    core, first = where_ref[0], where_ref[1]
    r = iota((256, 512), 0)
    own = turned(degree_ref[...].astype(F32), r // 32 * 64 + core * 32 + r % 32)
    orders = order_ref[...].astype(F32)
    for o in range(2):
        order = turned(orders, jnp.full((256, 256), first + o, jnp.int32))
        info_ref[:, o : o + 1] = (own >= order).astype(F32)
    q, col = iota((288, 384), 0), iota((288, 384), 1)
    hit = col == q % 48 // 12 * 72 + q // 48 * 12 + q % 12
    place_ref[...] = hit.astype(F32).astype(BF16)
    row, col = iota((288, 640), 0), iota((288, 640), 1)
    hit = col == row % 8 * 72 + row // 96 * 24 + row // 8 % 12
    pick_ref[...] = hit.astype(F32).astype(BF16)
    r = iota((256, 256), 0)
    order = turned(orders, r % 64 // 2 * 8 + r // 64 * 2 + r % 2)
    weight = jnp.where(order == 0, 1.0, 2.0)
    info_ref[:, 2:3] = 1.0 - 2.0 * (order - 2.0 * jnp.floor(order * 0.5))
    half = cos_ref.shape[1]
    count = 2 * half
    for at in range(0, half, 128):
        product = order * (iota((256, 128), 1) + at).astype(F32)
        phase = product - jnp.floor(product * (1.0 / count)) * count
        phase = jnp.where(phase < 0, phase + count, phase)
        phase = jnp.where(phase >= count, phase - count, phase)
        angle = phase * (2.0 * math.pi / count)
        cos_ref[:, at : at + 128] = (weight * jnp.cos(angle)).astype(BF16)
        sin_ref[:, at : at + 128] = (-weight * jnp.sin(angle)).astype(BF16)


def tables(where, order_map, degree_list, count):
    return pl.pallas_call(
        tables_kernel,
        out_shape=(
            jax.ShapeDtypeStruct((256, 3), F32),
            jax.ShapeDtypeStruct((288, 384), BF16),
            jax.ShapeDtypeStruct((288, 640), BF16),
            jax.ShapeDtypeStruct((256, count // 2), BF16),
            jax.ShapeDtypeStruct((256, count // 2), BF16),
        ),
        in_specs=[pl.BlockSpec(memory_space=pltpu.SMEM)]
        + [pl.BlockSpec(memory_space=pltpu.VMEM)] * 2,
        compiler_params=PARAMS,
        name="tables",
    )(where, order_map[None, :], degree_list[None, :])


def contract_kernel(x_ref, info_ref, keep_ref, send_ref):
    for o in range(2):
        table = x_ref[:, :, o * 256 : (o + 1) * 256].reshape(256, 256)
        table = jnp.where(info_ref[:, o : o + 1] > 0, table, jnp.zeros((), BF16))
        radial = x_ref[:, :, 512 + o * 512 : 1152 + o * 512].reshape(256, 640)
        partial = dot(radial, table, (0, 0))
        for ck in range(6):
            at = o * 64 + ck * 96
            keep_ref[o, ck * 48 : (ck + 1) * 48, :] = partial[at : at + 48, :]
            send_ref[o, ck * 48 : (ck + 1) * 48, :] = partial[at + 48 : at + 96, :].astype(BF16)


def contract(received, info):
    return pl.pallas_call(
        contract_kernel,
        out_shape=(
            jax.ShapeDtypeStruct((2, 288, 256), F32),
            jax.ShapeDtypeStruct((2, 288, 256), BF16),
        ),
        compiler_params=PARAMS,
        name="contract",
    )(received, info)


def join_kernel(keep_ref, other_ref, place_ref, out_ref):
    total = []
    for o in range(2):
        rows = (keep_ref[o] + other_ref[o].astype(F32)).astype(BF16)
        total.append(dot(rows, place_ref[...], (0, 0)))
    r, c = iota((64, 64), 0), iota((64, 64), 1)
    weave = (c == r % 2 * 32 + r // 2).astype(BF16)
    for ym in range(YM):
        halves = []
        for o in range(2):
            parts = [total[o][t * 32 : (t + 1) * 32, ym * 72 : (ym + 1) * 72] for t in range(8)]
            parts.append(jnp.zeros((32, 64), F32))
            halves.append(jnp.concatenate(parts, axis=1))
        pair = jnp.concatenate(halves, axis=0).astype(BF16)
        out_ref[ym * 64 : (ym + 1) * 64, :] = dot(weave, pair, (1, 0)).astype(BF16)


def join(keep, other, place):
    return pl.pallas_call(
        join_kernel,
        out_shape=jax.ShapeDtypeStruct((256, 640), BF16),
        compiler_params=PARAMS,
        name="join",
    )(keep, other, place)


def finish_kernel(x_ref, info_ref, pick_ref, cos_ref, sin_ref, vort_ref, out_hbm, out_ref, sems):
    x = x_ref[...].astype(F32)
    x = jnp.concatenate([x, x * info_ref[:, 2:3]], axis=0)
    lat = []
    for k in range(2):
        turned_x = jnp.concatenate([x[:, 12:], x[:, :12]], axis=1) if k else x
        rows = dot(pick_ref[...], turned_x.astype(BF16), (1, 1)).astype(BF16)
        lat.append(jnp.concatenate([rows[:, :256], rows[:, 256:]], axis=0))
    half = cos_ref.shape[1]
    copies = []
    for at in range(0, half, WIDTH):
        flow = dot(lat[0], cos_ref[:, at : at + WIDTH], (1, 0))
        flow += dot(lat[1], sin_ref[:, at : at + WIDTH], (1, 0))
        for h in range(2):
            span = slice(h * half + at, h * half + at + WIDTH)
            u = [flow[h * 288 + c * 96 : h * 288 + (c + 1) * 96] for c in range(3)]
            w = [vort_ref[c, :, span].astype(F32) for c in range(3)]
            for c in range(3):
                a, b = (c + 1) % 3, (c + 2) % 3
                out_ref[c, :, span] = (u[a] * w[b] - u[b] * w[a]).astype(BF16)
            part = pl.ds(h * half + at, WIDTH)
            copies.append(
                pltpu.make_async_copy(
                    out_ref.at[:, :, part], out_hbm.at[:, :, part], sems.at[len(copies)]
                )
            )
            copies[-1].start()
    for copy in copies:
        copy.wait()


def finish(rows, info, pick, cos, sin, vorticity):
    return pl.pallas_call(
        finish_kernel,
        out_shape=jax.ShapeDtypeStruct(vorticity.shape, BF16),
        out_specs=pl.BlockSpec(memory_space=pl.ANY),
        scratch_shapes=[
            pltpu.VMEM(vorticity.shape, BF16),
            pltpu.SemaphoreType.DMA((vorticity.shape[2] // WIDTH,)),
        ],
        compiler_params=PARAMS,
        name="finish",
    )(rows, info, pick, cos, sin, vorticity)


def shards(spectral, inverse, legendre, vorticity, degree_list, order_map):
    ym, core, mem = lax.axis_index("ym"), lax.axis_index("core"), lax.axis_index("mem")
    degrees = spectral.shape[0]
    packed = pack(
        spectral.reshape(degrees, 48, 192), inverse, jnp.transpose(legendre, (0, 2, 1))
    )
    received = lax.all_to_all(packed, ("ys", "ym"), 0, 0, tiled=True)
    where = jnp.stack([core, mem * 8 + ym * 2]).astype(jnp.int32)
    count = vorticity.shape[3]
    info, place, pick, cos, sin = tables(where, order_map, degree_list, count)
    keep, send = contract(received, info)
    other = lax.ppermute(send, "core", [(0, 1), (1, 0)])
    joined = join(keep, other, place)
    rows = lax.all_to_all(joined.reshape(128, 2, 640), ("ym", "mem"), 0, 0, tiled=True)

    field = jnp.transpose(vorticity, (0, 2, 1, 3)).reshape(3, 96, count)
    out = finish(rows.reshape(256, 640), info, pick, cos, sin, field)
    return jnp.transpose(out.reshape(3, 12, 8, count), (0, 2, 1, 3))


def solution(mesh):
    fine = Mesh(mesh.devices.reshape(YS, YM, CORES, 32), ("ys", "ym", "core", "mem"))
    grp = ("ys", "ym", "core")
    return jax.shard_map(
        shards,
        mesh=fine,
        in_specs=(
            P(grp, None, None, "mem", None),
            P(grp, None, None),
            P("mem", None, grp),
            P(None, "mem", grp, None),
            P(),
            P(),
        ),
        out_specs=P(None, "mem", grp, None),
        check_vma=False,
    )
```

time: 75.6 us -> 73.9 us (0.978)
  Pallas kernels: 14.7 us -> 12.5 us
  waiting for transfers between devices: 17.2 us -> 19.3 us
  local copies, waits for them, and re-layouts: 1.74 us -> 0.26 us
    all_to_all x1, waiting for transfers between devices: 15.8 us -> 18.1 us  [shards(): received = lax.all_to_all(packed, ('ys', 'ym'), 0, 0, tiled=True)]
    unnamed x14 -> x6, local copies, waits for them, and re-layouts: 1.49 us -> 0.01 us
    pallas_call x1, Pallas kernels: 3.47 us -> 2.1 us  [finish(): pl.pallas_call(finish_kernel, out_shape=jax.ShapeDtypeStruct(vorticity.sh...]
    pallas_call x1, Pallas kernels: 5.5 us -> 4.7 us  [tables(): pl.pallas_call(tables_kernel, out_shape=(jax.ShapeDtypeStruct((256, 3), F...]
    pallas_call x1, Pallas kernels: 1.23 us -> 0.47 us  [contract(): pl.pallas_call(contract_kernel, out_shape=(jax.ShapeDtypeStruct((2, 288,...]
  transfers between devices with their start and end apart: 2 -> 2, of which waited for: 2 -> 2; matrix products, arithmetic and copies ran while one was open for 0% -> 0% of each run, Pallas kernels for 7% -> 6%
where the time goes in v3:
time: 73.9 us; the launch traced here: 73.7 us
  blocking collectives  29.2 us (40%)
  waiting for transfers between devices  19.3 us (26%)
  Pallas kernels  12.5 us (17%)
  starting transfers between devices  12.3 us (17%)
    all_to_all x1, blocking collectives, shards(): lax.all_to_all(joined.reshape(128, 2, 640), ('ym', 'mem'), 0, 0, tiled=True)  29.2 us
    all_to_all x1, waiting for transfers between devices, shards(): received = lax.all_to_all(packed, ('ys', 'ym'), 0, 0, tiled=True)  18.1 us
    all_to_all x1, starting transfers between devices, shards(): received = lax.all_to_all(packed, ('ys', 'ym'), 0, 0, tiled=True)  7.79 us
    pallas_call x1, Pallas kernels, tables(): pl.pallas_call(tables_kernel, out_shape=(jax.ShapeDtypeStruct((256, 3), F...  4.7 us
    ppermute x1, starting transfers between devices, shards(): other = lax.ppermute(send, 'core', [(0, 1), (1, 0)])  4.52 us
    pallas_call x1, Pallas kernels, pack(): pl.pallas_call(pack_kernel, out_shape=jax.ShapeDtypeStruct((CHIPS, degree...  4.49 us
    pallas_call x1, Pallas kernels, finish(): pl.pallas_call(finish_kernel, out_shape=jax.ShapeDtypeStruct(vorticity.sh...  2.1 us
  transfers between devices with their start and end apart: 2, of which 2 were waited for; matrix products, arithmetic and copies ran while one was open for 0% of the time, Pallas kernels for 6%

profile of v3, /device:TPU:1, one launch (start us, length us, event | category | flops | bytes accessed | tf_op | source)
XLA Modules:
  0.0 73.7 jit_solution(9805687177641457875)
XLA Ops:
  0.0 0.0 copy-start.1
  0.0 0.0 copy-start.2
  0.0 4.5 %pack.1 = bf16[8,32,1664]{2,1,0:T(8,128)(2,1)} custom-call(bf16[32,48,192]{2,1,0:T(8,128)(2,1)} %bitcast.15, bf16[32,192,192]{2,1,0:T(8,128)(2,1)} %inv_hbm.1, bf16[8,32,256]{2,1,0:T(8,128)(2,1)} %bitcast.16), custom_call_target="tpu_custom_call" | custom-call | tf_op jit(solution)/shard_map/pack/pallas_call | solution.py:79
  4.5 0.0 copy-start
  4.5 7.8 %all-to-all-start = ((bf16[8,32,1664]{2,1,0:T(8,128)(2,1)}), bf16[8,32,1664]{2,1,0:T(8,128)(2,1)S(1)}, u32[]{:S(2)}, u32[]{:S(2)}) async-start(bf16[8,32,1664]{2,1,0:T(8,128)(2,1)} %pack.1), calls=%async_computation | async-start | bytes 1703936 | tf_op jit(solution)/shard_map/all_to_all | solution.py:251
  12.3 0.1 pad_add_fusion.where_ref
  12.4 0.0 copy-done.1
  12.4 0.0 copy-done.2
  12.4 4.7 %tables.1 = (f32[256,3]{1,0:T(8,128)S(1)}, bf16[288,384]{1,0:T(8,128)(2,1)S(1)}, bf16[288,640]{1,0:T(8,128)(2,1)S(1)}, bf16[256,768]{1,0:T(8,128)(2,1)S(1)}, bf16[256,768]{1,0:T(8,128)(2,1)S(1)}) custom-call(s32[2]{0:T(128)S(1)} %pad_add_fusion.where_ref, s32[1,256]{1,0:T(1,128)S(1)} %bitcast.14, s32[1,512]{1,0:T(1,128)S(1)} %bitcast.13), custom_call_target="tpu_custom_call" | custom-call | tf_op jit(solution)/shard_map/tables/pallas_call | solution.py:134
  17.1 18.1 %all-to-all-done.x_ref = bf16[8,32,1664]{2,1,0:T(8,128)(2,1)S(1)} async-done(((bf16[8,32,1664]{2,1,0:T(8,128)(2,1)}), bf16[8,32,1664]{2,1,0:T(8,128)(2,1)S(1)}, u32[]{:S(2)}, u32[]{:S(2)}) %all-to-all-start) | async-done | bytes 852000 | tf_op jit(solution)/shard_map/all_to_all | solution.py:251
  35.2 0.5 contract.1
  35.7 4.5 %collective-permute-start = (bf16[2,288,256]{2,1,0:T(8,128)(2,1)S(1)}, bf16[2,288,256]{2,1,0:T(8,128)(2,1)S(1)}, u32[]{:S(2)}, u32[]{:S(2)}) collective-permute-start(bf16[2,288,256]{2,1,0:T(8,128)(2,1)S(1)} %get-tuple-element.14), channel_id=1, source_target_pairs={{0,32},{32,0},{1,33},{33,1},{2,34},{34,2},{3,35},{35,3},{4,36},{36... | collective-permute-start | bytes 884744 | tf_op jit(solution)/shard_map/ppermute | solution.py:256
  40.2 1.2 %collective-permute-done.other_ref = bf16[2,288,256]{2,1,0:T(8,128)(2,1)S(1)} collective-permute-done((bf16[2,288,256]{2,1,0:T(8,128)(2,1)S(1)}, bf16[2,288,256]{2,1,0:T(8,128)(2,1)S(1)}, u32[]{:S(2)}, u32[]{:S(2)}) %collective-permute-start) | collective-permute-done | bytes 294944 | tf_op jit(solution)/shard_map/ppermute | solution.py:256
  41.4 0.7 join.1
  42.1 0.1 reshape.16
  42.3 29.2 %all_to_all.10 = bf16[128,2,640]{2,1,0:T(2,128)(2,1)S(1)} all-to-all(bf16[128,2,640]{2,1,0:T(2,128)(2,1)S(1)} %reshape.16), channel_id=1, replica_groups=mesh['ys'=2,'ym'=4,'core'=2,'mem'=32] {'ym','mem'}, dimensions={0} | all-to-all | bytes 655360 | tf_op jit(solution)/shard_map/all_to_all | solution.py:258
  71.5 0.1 reshape.17.x_ref
  71.6 0.0 copy-done
  71.6 2.1 %finish.1 = bf16[3,96,1536]{2,1,0:T(8,128)(2,1)} custom-call(bf16[256,640]{1,0:T(8,128)(2,1)S(1)} %reshape.17.x_ref, f32[256,3]{1,0:T(8,128)S(1)} %get-tuple-element.12.info_ref, bf16[288,640]{1,0:T(8,128)(2,1)S(1)} %get-tuple-element.16.pick_ref, bf16[256,768]{1,0:T(8,128)(2,1)S(1)} %get-tuple-element.17.cos_ref, ...), custom_call_target="tpu_custom_call" | custom-call | tf_op jit(solution)/shard_map/finish/pallas_call | solution.py:232
Async XLA Ops:
  0.0 12.4 %copy-start.1 = (s32[512]{0:T(512)S(1)}, s32[512]{0:T(512)}, u32[]{:S(2)}) copy-start(s32[512]{0:T(512)} %param.10) | copy-start | bytes 6148
  0.0 12.4 %copy-start.2 = (s32[256]{0:T(256)S(1)}, s32[256]{0:T(256)}, u32[]{:S(2)}) copy-start(s32[256]{0:T(256)} %param.11) | copy-start | bytes 3076
  4.5 67.1 %copy-start = (bf16[3,8,12,1536]{3,1,2,0:T(8,128)(2,1)S(1)}, bf16[3,8,12,1536]{3,1,2,0:T(8,128)(2,1)}, u32[]{:S(2)}) copy-start(bf16[3,8,12,1536]{3,1,2,0:T(8,128)(2,1)} %param.9) | copy-start | bytes 2654212
  4.5 30.7 %all-to-all-start = ((bf16[8,32,1664]{2,1,0:T(8,128)(2,1)}), bf16[8,32,1664]{2,1,0:T(8,128)(2,1)S(1)}, u32[]{:S(2)}, u32[]{:S(2)}) async-start(bf16[8,32,1664]{2,1,0:T(8,128)(2,1)} %pack.1), calls=%async_computation | async-start | bytes 1703936 | tf_op jit(solution)/shard_map/all_to_all | solution.py:251
  35.7 5.7 %collective-permute-start = (bf16[2,288,256]{2,1,0:T(8,128)(2,1)S(1)}, bf16[2,288,256]{2,1,0:T(8,128)(2,1)S(1)}, u32[]{:S(2)}, u32[]{:S(2)}) collective-permute-start(bf16[2,288,256]{2,1,0:T(8,128)(2,1)S(1)} %get-tuple-element.14), channel_id=1, source_target_pairs={{0,32},{32,0},{1,33},{33,1},{2,34},{34,2},{3,35},{35,3},{4,36},{36... | collective-permute-start | bytes 884744 | tf_op jit(solution)/shard_map/ppermute | solution.py:256

commit v4 on v3

--- a/solution.py
+++ b/solution.py
@@ -40,6 +40,9 @@
     r, c = iota((256, 256), 0), iota((256, 256), 1)
     turn = (r == c % 32 * 8 + c // 32).astype(BF16)
     swap = (c == r % degrees * 8 + r // degrees).astype(BF16)
+    r, c = iota((192, 192), 0), iota((192, 192), 1)
+    side = (r // 12 % 2 != lax.axis_index("core")).astype(jnp.int32)
+    near = (c == r // 96 * 96 + side * 48 + r % 96 // 24 * 12 + r % 12).astype(F32).astype(BF16)
     copies[0].wait()
     table = dot(leg_ref[...].reshape(rows, 256), turn, (1, 0)).astype(BF16)
     for chip in range(CHIPS):
@@ -53,9 +56,6 @@
             product = dot(spec_ref[l], inv_ref[l], (1, 1))
             for ck in range(6):
                 solved_ref[ck, l * 8 : (l + 1) * 8, :] = product[ck * 8 : (ck + 1) * 8, :]
-    r, c = iota((192, 192), 0), iota((192, 192), 1)
-    side = (r // 12 % 2 != lax.axis_index("core")).astype(jnp.int32)
-    near = (c == r // 96 * 96 + side * 48 + r % 96 // 24 * 12 + r % 12).astype(F32).astype(BF16)
     by_order = [dot(swap, solved_ref[ck].astype(BF16), (1, 0)).astype(BF16) for ck in range(6)]
     by_order = [dot(v, near, (1, 0)) for v in by_order]
     half = by_order[0].shape[1] // YS
@@ -156,7 +156,7 @@
         for ck in range(6):
             at = o * 64 + ck * 96
             keep_ref[o, ck * 48 : (ck + 1) * 48, :] = partial[at : at + 48, :]
-            send_ref[o, ck * 48 : (ck + 1) * 48, :] = partial[at + 48 : at + 96, :].astype(BF16)
+            send_ref[o, ck * 48 : (ck + 1) * 48, :] = partial[at + 48 : at + 96, :]
 
 
 def contract(received, info):
@@ -164,7 +164,7 @@
         contract_kernel,
         out_shape=(
             jax.ShapeDtypeStruct((2, 288, 256), F32),
-            jax.ShapeDtypeStruct((2, 288, 256), BF16),
+            jax.ShapeDtypeStruct((2, 288, 256), F32),
         ),
         compiler_params=PARAMS,
         name="contract",
@@ -174,7 +174,7 @@
 def join_kernel(keep_ref, other_ref, place_ref, out_ref):
     total = []
     for o in range(2):
-        rows = (keep_ref[o] + other_ref[o].astype(F32)).astype(BF16)
+        rows = (keep_ref[o] + other_ref[o]).astype(BF16)
         total.append(dot(rows, place_ref[...], (0, 0)))
     r, c = iota((64, 64), 0), iota((64, 64), 1)
     weave = (c == r % 2 * 32 + r // 2).astype(BF16)

time: 73.9 us -> 74.2 us (level)
  no operation moved by 1% of the time
where the time goes in v4:
time: 74.2 us; the launch traced here: 74 us
  blocking collectives  29.2 us (39%)
  waiting for transfers between devices  19.7 us (27%)
  Pallas kernels  12.3 us (17%)
  starting transfers between devices  12.3 us (17%)
    all_to_all x1, blocking collectives, shards(): lax.all_to_all(joined.reshape(128, 2, 640), ('ym', 'mem'), 0, 0, tiled=True)  29.2 us
    all_to_all x1, waiting for transfers between devices, shards(): received = lax.all_to_all(packed, ('ys', 'ym'), 0, 0, tiled=True)  18.1 us
    all_to_all x1, starting transfers between devices, shards(): received = lax.all_to_all(packed, ('ys', 'ym'), 0, 0, tiled=True)  7.78 us
    pallas_call x1, Pallas kernels, tables(): pl.pallas_call(tables_kernel, out_shape=(jax.ShapeDtypeStruct((256, 3), F...  4.7 us
    ppermute x1, starting transfers between devices, shards(): other = lax.ppermute(send, 'core', [(0, 1), (1, 0)])  4.53 us
    pallas_call x1, Pallas kernels, pack(): pl.pallas_call(pack_kernel, out_shape=jax.ShapeDtypeStruct((CHIPS, degree...  4.36 us
    pallas_call x1, Pallas kernels, finish(): pl.pallas_call(finish_kernel, out_shape=jax.ShapeDtypeStruct(vorticity.sh...  2.1 us
    ppermute x1, waiting for transfers between devices, shards(): other = lax.ppermute(send, 'core', [(0, 1), (1, 0)])  1.61 us
  transfers between devices with their start and end apart: 2, of which 2 were waited for; matrix products, arithmetic and copies ran while one was open for 0% of the time, Pallas kernels for 6%

profile of v4, /device:TPU:1, one launch (start us, length us, event | category | flops | bytes accessed | tf_op | source)
XLA Modules:
  0.0 74.0 jit_solution(4677351357077628740)
XLA Ops:
  0.0 0.0 copy-start.1
  0.0 0.0 copy-start.2
  0.0 4.4 %pack.1 = bf16[8,32,1664]{2,1,0:T(8,128)(2,1)} custom-call(bf16[32,48,192]{2,1,0:T(8,128)(2,1)} %bitcast.15, bf16[32,192,192]{2,1,0:T(8,128)(2,1)} %inv_hbm.1, bf16[8,32,256]{2,1,0:T(8,128)(2,1)} %bitcast.16), custom_call_target="tpu_custom_call" | custom-call | tf_op jit(solution)/shard_map/pack/pallas_call | solution.py:79
  4.4 0.0 copy-start
  4.4 7.8 %all-to-all-start = ((bf16[8,32,1664]{2,1,0:T(8,128)(2,1)}), bf16[8,32,1664]{2,1,0:T(8,128)(2,1)S(1)}, u32[]{:S(2)}, u32[]{:S(2)}) async-start(bf16[8,32,1664]{2,1,0:T(8,128)(2,1)} %pack.1), calls=%async_computation | async-start | bytes 1703936 | tf_op jit(solution)/shard_map/all_to_all | solution.py:251
  12.2 0.1 pad_add_fusion.where_ref
  12.2 0.0 copy-done.1
  12.2 0.0 copy-done.2
  12.2 4.7 %tables.1 = (f32[256,3]{1,0:T(8,128)S(1)}, bf16[288,384]{1,0:T(8,128)(2,1)S(1)}, bf16[288,640]{1,0:T(8,128)(2,1)S(1)}, bf16[256,768]{1,0:T(8,128)(2,1)S(1)}, bf16[256,768]{1,0:T(8,128)(2,1)S(1)}) custom-call(s32[2]{0:T(128)S(1)} %pad_add_fusion.where_ref, s32[1,256]{1,0:T(1,128)S(1)} %bitcast.14, s32[1,512]{1,0:T(1,128)S(1)} %bitcast.13), custom_call_target="tpu_custom_call" | custom-call | tf_op jit(solution)/shard_map/tables/pallas_call | solution.py:134
  16.9 18.1 %all-to-all-done.x_ref = bf16[8,32,1664]{2,1,0:T(8,128)(2,1)S(1)} async-done(((bf16[8,32,1664]{2,1,0:T(8,128)(2,1)}), bf16[8,32,1664]{2,1,0:T(8,128)(2,1)S(1)}, u32[]{:S(2)}, u32[]{:S(2)}) %all-to-all-start) | async-done | bytes 852000 | tf_op jit(solution)/shard_map/all_to_all | solution.py:251
  35.1 0.5 contract.1
  35.5 4.5 %collective-permute-start = (f32[2,288,256]{2,1,0:T(8,128)S(1)}, f32[2,288,256]{2,1,0:T(8,128)S(1)}, u32[]{:S(2)}, u32[]{:S(2)}) collective-permute-start(f32[2,288,256]{2,1,0:T(8,128)S(1)} %get-tuple-element.14), channel_id=1, source_target_pairs={{0,32},{32,0},{1,33},{33,1},{2,34},{34,2},{3,35},{35,3},{4,36},{36... | collective-permute-start | bytes 1769480 | tf_op jit(solution)/shard_map/ppermute | solution.py:256
  40.1 1.6 %collective-permute-done.other_ref = f32[2,288,256]{2,1,0:T(8,128)S(1)} collective-permute-done((f32[2,288,256]{2,1,0:T(8,128)S(1)}, f32[2,288,256]{2,1,0:T(8,128)S(1)}, u32[]{:S(2)}, u32[]{:S(2)}) %collective-permute-start) | collective-permute-done | bytes 589856 | tf_op jit(solution)/shard_map/ppermute | solution.py:256
  41.7 0.7 join.1
  42.4 0.1 reshape.16
  42.5 29.2 %all_to_all.10 = bf16[128,2,640]{2,1,0:T(2,128)(2,1)S(1)} all-to-all(bf16[128,2,640]{2,1,0:T(2,128)(2,1)S(1)} %reshape.16), channel_id=1, replica_groups=mesh['ys'=2,'ym'=4,'core'=2,'mem'=32] {'ym','mem'}, dimensions={0} | all-to-all | bytes 655360 | tf_op jit(solution)/shard_map/all_to_all | solution.py:258
  71.8 0.1 reshape.17.x_ref
  71.9 0.0 copy-done
  71.9 2.1 %finish.1 = bf16[3,96,1536]{2,1,0:T(8,128)(2,1)} custom-call(bf16[256,640]{1,0:T(8,128)(2,1)S(1)} %reshape.17.x_ref, f32[256,3]{1,0:T(8,128)S(1)} %get-tuple-element.12.info_ref, bf16[288,640]{1,0:T(8,128)(2,1)S(1)} %get-tuple-element.16.pick_ref, bf16[256,768]{1,0:T(8,128)(2,1)S(1)} %get-tuple-element.17.cos_ref, ...), custom_call_target="tpu_custom_call" | custom-call | tf_op jit(solution)/shard_map/finish/pallas_call | solution.py:232
Async XLA Ops:
  0.0 12.2 %copy-start.1 = (s32[512]{0:T(512)S(1)}, s32[512]{0:T(512)}, u32[]{:S(2)}) copy-start(s32[512]{0:T(512)} %param.10) | copy-start | bytes 6148
  0.0 12.2 %copy-start.2 = (s32[256]{0:T(256)S(1)}, s32[256]{0:T(256)}, u32[]{:S(2)}) copy-start(s32[256]{0:T(256)} %param.11) | copy-start | bytes 3076
  4.4 67.5 %copy-start = (bf16[3,8,12,1536]{3,1,2,0:T(8,128)(2,1)S(1)}, bf16[3,8,12,1536]{3,1,2,0:T(8,128)(2,1)}, u32[]{:S(2)}) copy-start(bf16[3,8,12,1536]{3,1,2,0:T(8,128)(2,1)} %param.9) | copy-start | bytes 2654212
  4.4 30.7 %all-to-all-start = ((bf16[8,32,1664]{2,1,0:T(8,128)(2,1)}), bf16[8,32,1664]{2,1,0:T(8,128)(2,1)S(1)}, u32[]{:S(2)}, u32[]{:S(2)}) async-start(bf16[8,32,1664]{2,1,0:T(8,128)(2,1)} %pack.1), calls=%async_computation | async-start | bytes 1703936 | tf_op jit(solution)/shard_map/all_to_all | solution.py:251
  35.5 6.1 %collective-permute-start = (f32[2,288,256]{2,1,0:T(8,128)S(1)}, f32[2,288,256]{2,1,0:T(8,128)S(1)}, u32[]{:S(2)}, u32[]{:S(2)}) collective-permute-start(f32[2,288,256]{2,1,0:T(8,128)S(1)} %get-tuple-element.14), channel_id=1, source_target_pairs={{0,32},{32,0},{1,33},{33,1},{2,34},{34,2},{3,35},{35,3},{4,36},{36... | collective-permute-start | bytes 1769480 | tf_op jit(solution)/shard_map/ppermute | solution.py:256

commit v5 on v4

--- a/solution.py
+++ b/solution.py
@@ -12,7 +12,7 @@
 CHIPS = YS * YM
 F32, BF16 = jnp.float32, jnp.bfloat16
 STEPS = 4
-WIDTH = 256
+WIDTH = 384
 PARAMS = pltpu.CompilerParams(vmem_limit_bytes=16 << 20)
 
 
@@ -156,7 +156,7 @@
         for ck in range(6):
             at = o * 64 + ck * 96
             keep_ref[o, ck * 48 : (ck + 1) * 48, :] = partial[at : at + 48, :]
-            send_ref[o, ck * 48 : (ck + 1) * 48, :] = partial[at + 48 : at + 96, :]
+            send_ref[o, ck * 48 : (ck + 1) * 48, :] = partial[at + 48 : at + 96, :].astype(BF16)
 
 
 def contract(received, info):
@@ -164,7 +164,7 @@
         contract_kernel,
         out_shape=(
             jax.ShapeDtypeStruct((2, 288, 256), F32),
-            jax.ShapeDtypeStruct((2, 288, 256), F32),
+            jax.ShapeDtypeStruct((2, 288, 256), BF16),
         ),
         compiler_params=PARAMS,
         name="contract",
@@ -174,7 +174,7 @@
 def join_kernel(keep_ref, other_ref, place_ref, out_ref):
     total = []
     for o in range(2):
-        rows = (keep_ref[o] + other_ref[o]).astype(BF16)
+        rows = (keep_ref[o] + other_ref[o].astype(F32)).astype(BF16)
         total.append(dot(rows, place_ref[...], (0, 0)))
     r, c = iota((64, 64), 0), iota((64, 64), 1)
     weave = (c == r % 2 * 32 + r // 2).astype(BF16)

time: 74.2 us -> 73.9 us (level)
  no operation moved by 1% of the time
where the time goes in v5:
time: 73.9 us; the launch traced here: 73.6 us
  blocking collectives  29.2 us (40%)
  waiting for transfers between devices  19.3 us (26%)
  Pallas kernels  12.4 us (17%)
  starting transfers between devices  12.3 us (17%)
    all_to_all x1, blocking collectives, shards(): lax.all_to_all(joined.reshape(128, 2, 640), ('ym', 'mem'), 0, 0, tiled=True)  29.2 us
    all_to_all x1, waiting for transfers between devices, shards(): received = lax.all_to_all(packed, ('ys', 'ym'), 0, 0, tiled=True)  18.1 us
    all_to_all x1, starting transfers between devices, shards(): received = lax.all_to_all(packed, ('ys', 'ym'), 0, 0, tiled=True)  7.78 us
    pallas_call x1, Pallas kernels, tables(): pl.pallas_call(tables_kernel, out_shape=(jax.ShapeDtypeStruct((256, 3), F...  4.7 us
    ppermute x1, starting transfers between devices, shards(): other = lax.ppermute(send, 'core', [(0, 1), (1, 0)])  4.53 us
    pallas_call x1, Pallas kernels, pack(): pl.pallas_call(pack_kernel, out_shape=jax.ShapeDtypeStruct((CHIPS, degree...  4.36 us
    pallas_call x1, Pallas kernels, finish(): pl.pallas_call(finish_kernel, out_shape=jax.ShapeDtypeStruct(vorticity.sh...  2.14 us
  transfers between devices with their start and end apart: 2, of which 2 were waited for; matrix products, arithmetic and copies ran while one was open for 0% of the time, Pallas kernels for 6%

profile of v5, /device:TPU:1, one launch (start us, length us, event | category | flops | bytes accessed | tf_op | source)
XLA Modules:
  0.0 73.6 jit_solution(17265189765702738749)
XLA Ops:
  0.0 0.0 copy-start.1
  0.0 0.0 copy-start.2
  0.0 4.4 %pack.1 = bf16[8,32,1664]{2,1,0:T(8,128)(2,1)} custom-call(bf16[32,48,192]{2,1,0:T(8,128)(2,1)} %bitcast.15, bf16[32,192,192]{2,1,0:T(8,128)(2,1)} %inv_hbm.1, bf16[8,32,256]{2,1,0:T(8,128)(2,1)} %bitcast.16), custom_call_target="tpu_custom_call" | custom-call | tf_op jit(solution)/shard_map/pack/pallas_call | solution.py:79
  4.4 0.0 copy-start
  4.4 7.8 %all-to-all-start = ((bf16[8,32,1664]{2,1,0:T(8,128)(2,1)}), bf16[8,32,1664]{2,1,0:T(8,128)(2,1)S(1)}, u32[]{:S(2)}, u32[]{:S(2)}) async-start(bf16[8,32,1664]{2,1,0:T(8,128)(2,1)} %pack.1), calls=%async_computation | async-start | bytes 1703936 | tf_op jit(solution)/shard_map/all_to_all | solution.py:251
  12.2 0.1 pad_add_fusion.where_ref
  12.2 0.0 copy-done.1
  12.2 0.0 copy-done.2
  12.2 4.7 %tables.1 = (f32[256,3]{1,0:T(8,128)S(1)}, bf16[288,384]{1,0:T(8,128)(2,1)S(1)}, bf16[288,640]{1,0:T(8,128)(2,1)S(1)}, bf16[256,768]{1,0:T(8,128)(2,1)S(1)}, bf16[256,768]{1,0:T(8,128)(2,1)S(1)}) custom-call(s32[2]{0:T(128)S(1)} %pad_add_fusion.where_ref, s32[1,256]{1,0:T(1,128)S(1)} %bitcast.14, s32[1,512]{1,0:T(1,128)S(1)} %bitcast.13), custom_call_target="tpu_custom_call" | custom-call | tf_op jit(solution)/shard_map/tables/pallas_call | solution.py:134
  16.9 18.1 %all-to-all-done.x_ref = bf16[8,32,1664]{2,1,0:T(8,128)(2,1)S(1)} async-done(((bf16[8,32,1664]{2,1,0:T(8,128)(2,1)}), bf16[8,32,1664]{2,1,0:T(8,128)(2,1)S(1)}, u32[]{:S(2)}, u32[]{:S(2)}) %all-to-all-start) | async-done | bytes 852000 | tf_op jit(solution)/shard_map/all_to_all | solution.py:251
  35.1 0.5 contract.1
  35.5 4.5 %collective-permute-start = (bf16[2,288,256]{2,1,0:T(8,128)(2,1)S(1)}, bf16[2,288,256]{2,1,0:T(8,128)(2,1)S(1)}, u32[]{:S(2)}, u32[]{:S(2)}) collective-permute-start(bf16[2,288,256]{2,1,0:T(8,128)(2,1)S(1)} %get-tuple-element.14), channel_id=1, source_target_pairs={{0,32},{32,0},{1,33},{33,1},{2,34},{34,2},{3,35},{35,3},{4,36},{36... | collective-permute-start | bytes 884744 | tf_op jit(solution)/shard_map/ppermute | solution.py:256
  40.1 1.2 %collective-permute-done.other_ref = bf16[2,288,256]{2,1,0:T(8,128)(2,1)S(1)} collective-permute-done((bf16[2,288,256]{2,1,0:T(8,128)(2,1)S(1)}, bf16[2,288,256]{2,1,0:T(8,128)(2,1)S(1)}, u32[]{:S(2)}, u32[]{:S(2)}) %collective-permute-start) | collective-permute-done | bytes 294944 | tf_op jit(solution)/shard_map/ppermute | solution.py:256
  41.3 0.7 join.1
  42.0 0.1 reshape.16
  42.1 29.2 %all_to_all.10 = bf16[128,2,640]{2,1,0:T(2,128)(2,1)S(1)} all-to-all(bf16[128,2,640]{2,1,0:T(2,128)(2,1)S(1)} %reshape.16), channel_id=1, replica_groups=mesh['ys'=2,'ym'=4,'core'=2,'mem'=32] {'ym','mem'}, dimensions={0} | all-to-all | bytes 655360 | tf_op jit(solution)/shard_map/all_to_all | solution.py:258
  71.4 0.1 reshape.17.x_ref
  71.5 0.0 copy-done
  71.5 2.1 %finish.1 = bf16[3,96,1536]{2,1,0:T(8,128)(2,1)} custom-call(bf16[256,640]{1,0:T(8,128)(2,1)S(1)} %reshape.17.x_ref, f32[256,3]{1,0:T(8,128)S(1)} %get-tuple-element.12.info_ref, bf16[288,640]{1,0:T(8,128)(2,1)S(1)} %get-tuple-element.16.pick_ref, bf16[256,768]{1,0:T(8,128)(2,1)S(1)} %get-tuple-element.17.cos_ref, ...), custom_call_target="tpu_custom_call" | custom-call | tf_op jit(solution)/shard_map/finish/pallas_call | solution.py:232
Async XLA Ops:
  0.0 12.2 %copy-start.1 = (s32[512]{0:T(512)S(1)}, s32[512]{0:T(512)}, u32[]{:S(2)}) copy-start(s32[512]{0:T(512)} %param.10) | copy-start | bytes 6148
  0.0 12.2 %copy-start.2 = (s32[256]{0:T(256)S(1)}, s32[256]{0:T(256)}, u32[]{:S(2)}) copy-start(s32[256]{0:T(256)} %param.11) | copy-start | bytes 3076
  4.4 67.1 %copy-start = (bf16[3,8,12,1536]{3,1,2,0:T(8,128)(2,1)S(1)}, bf16[3,8,12,1536]{3,1,2,0:T(8,128)(2,1)}, u32[]{:S(2)}) copy-start(bf16[3,8,12,1536]{3,1,2,0:T(8,128)(2,1)} %param.9) | copy-start | bytes 2654212
  4.4 30.7 %all-to-all-start = ((bf16[8,32,1664]{2,1,0:T(8,128)(2,1)}), bf16[8,32,1664]{2,1,0:T(8,128)(2,1)S(1)}, u32[]{:S(2)}, u32[]{:S(2)}) async-start(bf16[8,32,1664]{2,1,0:T(8,128)(2,1)} %pack.1), calls=%async_computation | async-start | bytes 1703936 | tf_op jit(solution)/shard_map/all_to_all | solution.py:251
  35.5 5.7 %collective-permute-start = (bf16[2,288,256]{2,1,0:T(8,128)(2,1)S(1)}, bf16[2,288,256]{2,1,0:T(8,128)(2,1)S(1)}, u32[]{:S(2)}, u32[]{:S(2)}) collective-permute-start(bf16[2,288,256]{2,1,0:T(8,128)(2,1)S(1)} %get-tuple-element.14), channel_id=1, source_target_pairs={{0,32},{32,0},{1,33},{33,1},{2,34},{34,2},{3,35},{35,3},{4,36},{36... | collective-permute-start | bytes 884744 | tf_op jit(solution)/shard_map/ppermute | solution.py:256
